TPU v7x, 32 devices: a whole 2x2x4 slice. The times are simulated.
32 devices in a mesh: dp: 8 (over z, x), head: 4 (over y, core).
Axes of the slice: x: 2, y: 2, z: 4, core: 2. Of those that a mesh axis runs over, the one named last changes fastest.
Arguments:
- layer_input: bfloat16 [64, 197, 768], P(('dp', 'head')), may hold values from -6 to 6
- prompts: bfloat16 [100, 768], replicated, may hold values from -6 to 6
- lengths: int32 [64], P('dp'), may hold values from 1 to 100, as said below
- key_mask: int32 [64, 297], P('dp'), may hold values 0 or 1
- ln1_gain: float32 [768], replicated, may hold values from 0.1 to 1.9
- ln1_shift: float32 [768], replicated, may hold values from -1.5 to 1.5
- w_qkv: bfloat16 [3, 768, 768], P(None, 'dp', 'head'), may hold values from -0.3125 to 0.3125
- w_out: bfloat16 [768, 768], P('head', 'dp'), may hold values from -0.875 to 0.875
- b_out: float32 [768], replicated, may hold values from -1.5 to 1.5
- ln2_gain: float32 [768], replicated, may hold values from 0.1 to 1.9
- ln2_shift: float32 [768], replicated, may hold values from -1.5 to 1.5
- w_fc1: bfloat16 [768, 3072], P('dp', 'head'), may hold values from -0.21875 to 0.21875
- b_fc1: float32 [3072], P('head'), may hold values from -2.5 to 2.5
- w_fc2: bfloat16 [3072, 768], P('head', 'dp'), may hold values from -0.15625 to 0.15625
- b_fc2: float32 [768], replicated, may hold values from -1.5 to 1.5
- grad_output: bfloat16 [64, 297, 768], P(('dp', 'head')), may hold values from -6 to 6
Outputs:
- layer_output: bfloat16 [64, 297, 768], P(('dp', 'head'))
- grad_input: bfloat16 [64, 197, 768], P(('dp', 'head'))
- grad_prompts: float32 [100, 768], replicated
Inputs may be any that keep to these rules, and one draw needn't show every extreme that they name: `lengths`: each length is one of 1, 10, 50 and 100; both 1 and 100 occur.
All inputs are finite; a program needn't handle non-finite values. No bound on the sum of `key_mask` on one device may be relied on, other than what follows from the above.
Results may differ from a plain program's by a relative error of at most 0.019.
Values may be sent and summed in bfloat16 or wider, within the bound.
No kernel may reach another device: no remote copies, remote signals or barrier semaphores. Data moves between devices by JAX's collectives and lax.ppermute only.
A program may use at most 128 MiB of HBM per device.

v0:
```python
import jax
import jax.numpy as jnp
from jax import lax
from jax.sharding import PartitionSpec as P

HEAD_DIM = 64
IMG_TOK = 197
PROMPTS = 100


EPSILON = 1e-06


def layer_norm(rows, gain, shift):
    center = rows - jnp.mean(rows, axis=-1, keepdims=True)
    return (
        center * lax.rsqrt(jnp.mean(center * center, axis=-1, keepdims=True) + EPSILON) * gain
        + shift
    )


def token_masks(lengths, key_mask):
    position = lax.broadcasted_iota(jnp.int32, key_mask.shape, 1)
    used = (position < IMG_TOK) | (position - IMG_TOK < lengths[:, None])
    seen = (key_mask == 1) | (position == 0)
    return (used, used & seen)


def project(rows_b, weight):
    return jnp.einsum("isd,dc->isc", rows_b, weight, preferred_element_type=jnp.float32)


def attend(rows_b, full_qkv, visible):
    img_count, seq_len = (rows_b.shape[0], rows_b.shape[1])
    head_count = full_qkv.shape[2] // HEAD_DIM
    projected = jnp.einsum(
        "isd,tdc->tisc", rows_b, full_qkv, preferred_element_type=jnp.float32
    ).astype(jnp.bfloat16)
    projected = projected.reshape(3, img_count, seq_len, head_count, HEAD_DIM)
    query_rows, key_rows, value_rows = (projected[0], projected[1], projected[2])
    scores = jnp.einsum(
        "ishc,ithc->ihst", query_rows, key_rows, preferred_element_type=jnp.float32
    ) * HEAD_DIM ** (-0.5)
    scores = jnp.where(visible[:, None, None, :], scores, -1000000000.0)
    attn_probs = jax.nn.softmax(scores, axis=-1)
    return (query_rows, key_rows, value_rows, attn_probs)


def mix_values(probs_b, value_rows):
    img_count, seq_len = (value_rows.shape[0], value_rows.shape[1])
    context = jnp.einsum("ihst,ithc->ishc", probs_b, value_rows, preferred_element_type=jnp.float32)
    return context.astype(jnp.bfloat16).reshape(img_count, seq_len, value_rows.shape[2] * HEAD_DIM)


def mlp_back(grad_all, pre_act, fc1_rows, fc2_rows):
    grad_active_b = jnp.einsum(
        "isd,fd->isf", grad_all, fc2_rows, preferred_element_type=jnp.float32
    ).astype(jnp.bfloat16)
    _, gelu_back = jax.vjp(lambda values_in: jax.nn.gelu(values_in, approximate=False), pre_act)
    grad_pre_b = gelu_back(grad_active_b.astype(jnp.float32))[0].astype(jnp.bfloat16)
    return jnp.einsum("isf,df->isd", grad_pre_b, fc1_rows, preferred_element_type=jnp.float32)


def attn_back(grad_all, out_rows, qkv_rows, query_rows, key_rows, value_rows, attn_probs, probs_b):
    img_count, seq_len, head_count = (value_rows.shape[0], value_rows.shape[1], value_rows.shape[2])
    local_width = head_count * HEAD_DIM
    grad_context = jnp.einsum(
        "isd,cd->isc", grad_all, out_rows, preferred_element_type=jnp.float32
    ).astype(jnp.bfloat16)
    grad_context = grad_context.reshape(img_count, seq_len, head_count, HEAD_DIM)
    grad_value = jnp.einsum(
        "ihst,ishc->ithc", probs_b, grad_context, preferred_element_type=jnp.float32
    ).astype(jnp.bfloat16)
    grad_probs = jnp.einsum(
        "ishc,ithc->ihst", grad_context, value_rows, preferred_element_type=jnp.float32
    )
    grad_scores = (
        attn_probs * (grad_probs - jnp.sum(attn_probs * grad_probs, axis=-1, keepdims=True))
    ).astype(jnp.bfloat16)
    grad_query = (
        jnp.einsum("ihst,ithc->ishc", grad_scores, key_rows, preferred_element_type=jnp.float32)
        * HEAD_DIM ** (-0.5)
    ).astype(jnp.bfloat16)
    grad_key = (
        jnp.einsum("ihst,ishc->ithc", grad_scores, query_rows, preferred_element_type=jnp.float32)
        * HEAD_DIM ** (-0.5)
    ).astype(jnp.bfloat16)
    stacked = jnp.stack([grad_query, grad_key, grad_value]).reshape(
        3, img_count, seq_len, local_width
    )
    return jnp.einsum("tisc,tdc->isd", stacked, qkv_rows, preferred_element_type=jnp.float32)


def per_device(
    layer_input,
    prompts,
    lengths,
    key_mask,
    ln1_gain,
    ln1_shift,
    w_qkv,
    w_out,
    b_out,
    ln2_gain,
    ln2_shift,
    w_fc1,
    b_fc1,
    w_fc2,
    b_fc2,
    grad_output,
):
    own_count = layer_input.shape[0]
    model_width = layer_input.shape[2]
    offset = lax.axis_index("head") * own_count
    used_all, visible = token_masks(lengths, key_mask)
    used_own = lax.dynamic_slice_in_dim(used_all, offset, own_count, 0).astype(jnp.float32)[
        ..., None
    ]
    gain_one, shift_one = (ln1_gain, ln1_shift)
    gain_two, shift_two = (ln2_gain, ln2_shift)
    full_qkv, full_out, full_fc1, full_fc2 = (
        lax.all_gather(w_qkv, "dp", axis=1, tiled=True),
        lax.all_gather(w_out, "dp", axis=1, tiled=True),
        lax.all_gather(w_fc1, "dp", axis=0, tiled=True),
        lax.all_gather(w_fc2, "dp", axis=1, tiled=True),
    )
    prompt_rows = jnp.broadcast_to(
        prompts.astype(jnp.float32)[None], (own_count, PROMPTS, model_width)
    )
    stream = jnp.concatenate([layer_input.astype(jnp.float32), prompt_rows], axis=1)
    normed_attn, back_attn_norm = jax.vjp(
        lambda rows: layer_norm(rows, gain_one, shift_one), stream
    )
    normed_attn_b = normed_attn.astype(jnp.bfloat16)
    grad_rows = grad_output.astype(jnp.float32) * used_own
    gathered_attn = lax.all_gather(normed_attn_b, "head", axis=0, tiled=True)
    query_rows, key_rows, value_rows, attn_probs = attend(gathered_attn, full_qkv, visible)
    probs_b = attn_probs.astype(jnp.bfloat16)
    context = mix_values(probs_b, value_rows)
    attn_sum = lax.psum_scatter(
        project(context, full_out).astype(jnp.bfloat16), "head", scatter_dimension=0, tiled=True
    ).astype(jnp.float32)
    hidden_mid = stream + attn_sum + b_out
    normed_mlp, back_mlp_norm = jax.vjp(
        lambda rows: layer_norm(rows, gain_two, shift_two), hidden_mid
    )
    normed_mlp_b = normed_mlp.astype(jnp.bfloat16)
    gathered_mlp = lax.all_gather(normed_mlp_b, "head", axis=0, tiled=True)
    pre_act = project(gathered_mlp, full_fc1) + b_fc1
    active_b = jax.nn.gelu(pre_act, approximate=False).astype(jnp.bfloat16)
    mlp_sum = lax.psum_scatter(
        project(active_b, full_fc2).astype(jnp.bfloat16), "head", scatter_dimension=0, tiled=True
    ).astype(jnp.float32)
    result = ((hidden_mid + mlp_sum + b_fc2) * used_own).astype(jnp.bfloat16)
    held_inputs = lax.optimization_barrier((w_qkv, w_out, w_fc1, w_fc2, grad_rows))
    grad_rows = held_inputs[4]
    back_qkv, back_out, back_fc1, back_fc2 = (
        lax.all_gather(held_inputs[0], "dp", axis=1, tiled=True),
        lax.all_gather(held_inputs[1], "dp", axis=1, tiled=True),
        lax.all_gather(held_inputs[2], "dp", axis=0, tiled=True),
        lax.all_gather(held_inputs[3], "dp", axis=1, tiled=True),
    )
    grad_mlp_b = grad_rows.astype(jnp.bfloat16)
    grad_mlp_all, gathered_again = (
        lax.all_gather(grad_mlp_b, "head", axis=0, tiled=True),
        lax.all_gather(normed_mlp_b, "head", axis=0, tiled=True),
    )
    pre_act = project(gathered_again, back_fc1) + b_fc1
    grad_normed_mlp = lax.psum_scatter(
        mlp_back(grad_mlp_all, pre_act, back_fc1, back_fc2).astype(jnp.bfloat16),
        "head",
        scatter_dimension=0,
        tiled=True,
    ).astype(jnp.float32)
    grad_mid = grad_rows + back_mlp_norm(grad_normed_mlp)[0]
    grad_attn_b = grad_mid.astype(jnp.bfloat16)
    grad_attn_all, gathered_again = (
        lax.all_gather(grad_attn_b, "head", axis=0, tiled=True),
        lax.all_gather(normed_attn_b, "head", axis=0, tiled=True),
    )
    query_rows, key_rows, value_rows, attn_probs = attend(gathered_again, back_qkv, visible)
    probs_b = attn_probs.astype(jnp.bfloat16)
    grad_partial = attn_back(
        grad_attn_all, back_out, back_qkv, query_rows, key_rows, value_rows, attn_probs, probs_b
    )
    grad_normed_attn = lax.psum_scatter(
        grad_partial.astype(jnp.bfloat16), "head", scatter_dimension=0, tiled=True
    ).astype(jnp.float32)
    grad_stream = grad_mid + back_attn_norm(grad_normed_attn)[0]
    grad_input = grad_stream[:, :IMG_TOK].astype(jnp.bfloat16)
    grad_prompts = lax.psum(jnp.sum(grad_stream[:, IMG_TOK:], axis=0), ("dp", "head"))
    return (result, grad_input, grad_prompts)


def solution(mesh):
    placed = (
        P(("dp", "head"), None, None),
        P(),
        P("dp"),
        P("dp", None),
        P(),
        P(),
        P(None, "dp", "head"),
        P("head", "dp"),
        P(),
        P(),
        P(),
        P("dp", "head"),
        P("head"),
        P("head", "dp"),
        P(),
        P(("dp", "head"), None, None),
    )
    return jax.shard_map(
        per_device,
        mesh=mesh,
        in_specs=placed,
        out_specs=(P(("dp", "head"), None, None), P(("dp", "head"), None, None), P()),
        check_vma=False,
    )
```

profile of v0, /device:TPU:0, one launch (start us, length us, event | category | flops | bytes accessed | tf_op | source)
XLA Modules:
  0.0 716.9 jit_solution(3644398181313778874)
XLA Ops:
  10.9 1.3 add_convert_fusion.1
  12.6 40.5 %all_gather.39 = bf16[3,768,192]{2,0,1:T(4,128)(2,1)} all-gather(bf16[3,96,192]{2,0,1:T(4,128)(2,1)S(1)} %copy.34), channel_id=1, replica_groups=mesh['dp'=8,'head'=4] {'dp'}, dimensions={1}, use_global_device_ids=true | all-gather | bytes 995328 | tf_op jit(solution)/shard_map/all_gather | solution.py:122
  53.1 3.4 copy.35
  56.5 31.0 %all_gather.40 = bf16[192,768]{0,1:T(8,128)(2,1)S(1)} all-gather(bf16[192,96]{0,1:T(8,128)(2,1)S(1)} %copy.37), channel_id=1, replica_groups=mesh['dp'=8,'head'=4] {'dp'}, dimensions={1}, use_global_device_ids=true | all-gather | bytes 331776 | tf_op jit(solution)/shard_map/all_gather | solution.py:123
  87.6 5.2 convert_bitcast_fusion.1
  92.8 1.9 fusion.167
  94.7 8.2 %fusion.168 = (f32[8,3,297]{2,1,0:T(4,128)S(1)}, f32[8,3,297,297]{2,3,1,0:T(8,128)}) fusion(pred[8,297]{1,0:T(8,128)(4,1)S(1)} %get-tuple-element.30, bf16[8,297,3,64]{1,3,2,0:T(8,128)(2,1)} %bitcast.105, bf16[8,297,3,64]{1,3,2,0:T(8,128)(2,1)} %bitcast.104), kind=kOutput, calls=%fused_computation.222 | convolution fusion | flops 279446432 | bytes 10323720 | tf_op jit(solution)/shard_map/sub | solution.py:45
  102.9 5.8 fusion.73
  108.7 3.2 convolution_convert_fusion
  113.1 1.5 convert_multiply_fusion.4
  114.6 38.6 %reduce-scatter.5.cloned.1.call-done = bf16[2,297,768]{2,1,0:T(8,128)(2,1)} async-done(((bf16[8,297,768]{2,1,0:T(8,128)(2,1)}), bf16[2,297,768]{2,1,0:T(8,128)(2,1)}) %reduce-scatter.5.cloned.1.call-update) | async-done | bytes 912400 | tf_op jit(solution)/shard_map/reduce_scatter | solution.py:140
  153.3 1.6 fusion.165
  154.9 1.7 multiply_reduce_fusion.3
  156.7 1.5 add_convert_fusion
  158.8 2.6 convert_element_type.129
  163.2 26.8 %all-gather.11.cloned.1.call-done = bf16[8,297,768]{2,1,0:T(8,128)(2,1)} async-done(((bf16[2,297,768]{2,1,0:T(8,128)(2,1)}), bf16[8,297,768]{2,1,0:T(8,128)(2,1)}) %all-gather.11.cloned.1.call-update) | async-done | bytes 3649552 | tf_op jit(solution)/shard_map/all_gather | solution.py:148
  190.0 8.4 %fusion.82 = f32[8,297,768]{2,1,0:T(8,128)} fusion(bf16[8,297,768]{2,1,0:T(8,128)(2,1)} %all-gather.11.cloned.1.call-done, bf16[768,768]{1,0:T(8,128)(2,1)} %all-gather.17.cloned.1.call-done), kind=kOutput, calls=%fused_computation.120 | convolution fusion | flops 2802843648 | bytes 12128256 | tf_op jit(solution)/shard_map/isd,dc->isc/dot_general | solution.py:30
  198.4 35.4 %all-gather.21.cloned.1.call-done = bf16[768,768]{0,1:T(8,128)(2,1)} async-done(((bf16[768,96]{0,1:T(8,128)(2,1)}), bf16[768,768]{0,1:T(8,128)(2,1)}) %all-gather.21.cloned.1.call-update) | async-done | bytes 1179664 | tf_op jit(solution)/shard_map/all_gather | solution.py:161
  233.8 31.9 %all-gather.19.cloned.1.call-done = bf16[8,297,768]{2,1,0:T(8,128)(2,1)} async-done(((bf16[2,297,768]{2,1,0:T(8,128)(2,1)}), bf16[8,297,768]{2,1,0:T(8,128)(2,1)}) %all-gather.19.cloned.1.call-update) | async-done | bytes 3649552 | tf_op jit(solution)/shard_map/all_gather | solution.py:165
  265.8 27.0 %fusion.57 = bf16[8,297,768]{2,1,0:T(8,128)(2,1)} fusion(f32[8,297,768]{2,1,0:T(8,128)} %fusion.82, f32[768]{0:T(1024)S(1)} %copy-done.35, bf16[8,297,768]{2,1,0:T(8,128)(2,1)} %all-gather.19.cloned.1.call-done, bf16[768,768]{0,1:T(8,128)(2,1)} %all-gather.21.cloned.1.call-done, bf16[768,768]{1,0:T(8,128)(2,1)} %all-gather.17.cloned.1.call-done), kind=kOutput, calls=%fused_computation.89 | convolution fusion | flops 5744369664 | bytes 16960512 | tf_op jit(solution)/shard_map/isf,df->isd/dot_general | solution.py:61
  292.7 9.2 %reduce-scatter.7.cloned.1.call-start = ((), (), s32[]{:S(2)}) async-start(), calls=%async_computation.9 | async-start | bytes 4669440 | tf_op jit(solution)/shard_map/reduce_scatter | solution.py:151
  301.9 7.6 %all-gather.13.cloned.1.call-done = bf16[768,768]{1,0:T(8,128)(2,1)} async-done(((bf16[96,768]{1,0:T(8,128)(2,1)}), bf16[768,768]{1,0:T(8,128)(2,1)}) %all-gather.13.cloned.1.call-update) | async-done | bytes 1179664 | tf_op jit(solution)/shard_map/all_gather | solution.py:124
  309.5 10.9 %fusion.70 = (u8[297,768]{1,0:T(8,128)(4,1)S(1)}, u8[297,768]{1,0:T(8,128)(4,1)S(1)}, f32[8,297,768]{2,1,0:T(8,128)}) fusion(f32[768]{0:T(1024)S(1)} %copy-done.35, bf16[8,297,768]{2,1,0:T(8,128)(2,1)} %all-gather.11.cloned.1.call-done, bf16[768,768]{1,0:T(8,128)(2,1)} %all-gather.13.cloned.1.call-done), kind=kOutput, calls=%fused_computation.109 | convolution fusion | flops 2827934208 | bytes 12587520 | tf_op jit(solution)/shard_map/isd,dc->isc/dot_general | solution.py:30
  320.4 31.4 %all-gather.15.cloned.1.call-done = bf16[768,768]{0,1:T(8,128)(2,1)} async-done(((bf16[768,96]{0,1:T(8,128)(2,1)}), bf16[768,768]{0,1:T(8,128)(2,1)}) %all-gather.15.cloned.1.call-update) | async-done | bytes 1179664 | tf_op jit(solution)/shard_map/all_gather | solution.py:125
  351.8 23.0 %fusion.60 = bf16[8,297,768]{2,1,0:T(8,128)(2,1)} fusion(f32[8,297,768]{2,1,0:T(8,128)} %get-tuple-element.33, f32[768]{0:T(1024)S(1)} %copy-done.35, bf16[768,768]{0,1:T(8,128)(2,1)} %all-gather.15.cloned.1.call-done, u8[297,768]{1,0:T(8,128)(4,1)S(1)} %get-tuple-element.20, u8[297,768]{1,0:T(8,128)(4,1)S(1)} %get-tuple-element.19), kind=kOutput, calls=%fused_computation.90 | convolution fusion | flops 2934226944 | bytes 12587520 | tf_op jit(solution)/shard_map/isd,dc->isc/dot_general | solution.py:30
  375.0 1.9 multiply_reduce_fusion.2
  377.9 37.2 %reduce-scatter.7.cloned.1.call-done = bf16[2,297,768]{2,1,0:T(8,128)(2,1)} async-done(((bf16[8,297,768]{2,1,0:T(8,128)(2,1)}), bf16[2,297,768]{2,1,0:T(8,128)(2,1)}) %reduce-scatter.7.cloned.1.call-update) | async-done | bytes 912400 | tf_op jit(solution)/shard_map/reduce_scatter | solution.py:151
  415.1 3.6 fusion.164
  419.0 31.3 %all_gather.49 = bf16[192,768]{0,1:T(8,128)(2,1)S(1)} all-gather(bf16[192,96]{0,1:T(8,128)(2,1)S(1)} %copy.42), channel_id=1, replica_groups=mesh['dp'=8,'head'=4] {'dp'}, dimensions={1}, use_global_device_ids=true | all-gather | bytes 331776 | tf_op jit(solution)/shard_map/all_gather | solution.py:159
  450.3 39.0 %all_gather.47 = bf16[3,768,192]{2,0,1:T(4,128)(2,1)S(1)} all-gather(bf16[3,96,192]{2,0,1:T(4,128)(2,1)S(1)} %copy.40), channel_id=1, replica_groups=mesh['dp'=8,'head'=4] {'dp'}, dimensions={1}, use_global_device_ids=true | all-gather | bytes 995328 | tf_op jit(solution)/shard_map/all_gather | solution.py:158
  489.3 7.7 %convert_bitcast_fusion = bf16[3,8,297,192]{2,3,1,0:T(8,128)(2,1)S(1)} fusion(bf16[8,297,768]{2,1,0:T(8,128)(2,1)} %all-gather.9.cloned.1.call-done, bf16[3,768,192,1]{2,0,1,3:T(4,128)(2,1)S(1)} %bitcast.101), kind=kOutput, calls=%fused_computation.84 | convolution fusion | flops 2103501312 | bytes 7271424 | tf_op jit(solution)/shard_map/isd,tdc->tisc/dot_general | solution.py:36
  497.1 2.0 fusion.166
  499.1 8.2 %fusion.169 = (f32[8,3,297]{2,1,0:T(4,128)S(1)}, f32[8,3,297,297]{2,3,1,0:T(8,128)}) fusion(pred[8,297]{1,0:T(8,128)(4,1)S(1)} %copy-done.33, bf16[8,297,3,64]{1,3,2,0:T(8,128)(2,1)} %bitcast.98, bf16[8,297,3,64]{1,3,2,0:T(8,128)(2,1)} %bitcast.96), kind=kOutput, calls=%fused_computation.223 | convolution fusion | flops 279446432 | bytes 10323720 | tf_op jit(solution)/shard_map/sub | solution.py:45
  507.3 3.6 convolution_convert_fusion.1
  511.0 7.6 %fusion.74 = bf16[8,3,64,297]{3,2,1,0:T(8,128)(2,1)} fusion(bf16[8,297,3,64]{1,3,2,0:T(8,128)(2,1)S(1)} %bitcast.109, f32[8,3,297,297]{2,3,1,0:T(8,128)} %get-tuple-element.35, f32[8,3,297]{2,1,0:T(4,128)S(1)} %get-tuple-element.34), kind=kOutput, calls=%fused_computation.113 | convolution fusion | flops 275668288 | bytes 10321344 | tf_op jit(solution)/shard_map/ihst,ishc->ithc/dot_general | solution.py:71
  518.7 3.4 multiply_reduce_fusion
  522.0 1.7 multiply_convert_fusion
  523.7 3.3 multiply_convert_fusion.1
  528.8 5.4 bitcast_convert_fusion
  534.3 40.0 %reduce-scatter.11.cloned.1.call-done = bf16[2,297,768]{2,1,0:T(8,128)(2,1)} async-done(((bf16[8,297,768]{2,1,0:T(8,128)(2,1)}), bf16[2,297,768]{2,1,0:T(8,128)(2,1)}) %reduce-scatter.11.cloned.1.call-update) | async-done | bytes 912400 | tf_op jit(solution)/shard_map/reduce_scatter | solution.py:186
  574.3 1.8 multiply_reduce_fusion.1
  576.2 1.9 fusion.92
  578.2 1.6 add_add_fusion.2
  581.9 2.8 copy.51
  584.7 1.3 slice.49
  586.1 1.3 copy.52
  587.4 120.3 %all-reduce.2.cloned.1.call-done = f32[100,768]{1,0:T(8,128)} async-done(((f32[100,768]{1,0:T(8,128)}), f32[100,768]{1,0:T(8,128)}) %all-reduce.2.cloned.1.call-update) | async-done | bytes 307216 | tf_op jit(solution)/shard_map/psum | solution.py:191
  707.7 1.7 copy.75
  (135 shorter events, 12.2 us)
Async XLA Ops:
  8.0 2.8 copy-start.18
  8.0 2.8 copy-start.29
  8.0 79.6 %all-gather.9.cloned.1.call-start = ((), (), s32[]{:S(2)}) async-start(), calls=%async_computation.4 | async-start | bytes 4669440 | tf_op jit(solution)/shard_map/all_gather | solution.py:136
  10.2 2.1 copy-start.13
  10.2 2.2 copy-start.10
  10.4 1.9 copy-start.15
  12.2 75.3 %copy-start.28 = (s32[8,297]{1,0:T(8,128)S(1)}, s32[8,297]{1,0:T(8,128)}, u32[]{:S(2)}) copy-start(s32[8,297]{1,0:T(8,128)} %param.19) | copy-start | bytes 28516
  12.2 75.3 %copy-start.34 = (s32[8]{0:T(128)S(1)}, s32[8]{0:T(128)}, u32[]{:S(2)}) copy-start(s32[8]{0:T(128)} %param.18) | copy-start | bytes 100
  12.2 141.0 %reduce-scatter.5.cloned.1.call-start = ((), (), s32[]{:S(2)}) async-start(), calls=%async_computation.5 | async-start | bytes 4669440 | tf_op jit(solution)/shard_map/reduce_scatter | solution.py:140
  87.6 7.2 copy-start.32
  111.9 41.3 %copy-start.12 = (f32[768]{0:T(1024)S(1)}, f32[768]{0:T(1024)}, u32[]{:S(2)}) copy-start(f32[768]{0:T(1024)} %param.24) | copy-start | bytes 9220
  112.0 51.3 %all-gather.17.cloned.1.call-start = ((), (), s32[]{:S(2)}) async-start(), calls=%async_computation.10 | async-start | bytes 1327104 | tf_op jit(solution)/shard_map/all_gather | solution.py:160
  114.6 42.1 %copy-start.17 = (f32[768]{0:T(1024)S(1)}, f32[768]{0:T(1024)}, u32[]{:S(2)}) copy-start(f32[768]{0:T(1024)} %param.25) | copy-start | bytes 9220
  114.6 42.1 %copy-start.30 = (f32[768]{0:T(1024)S(1)}, f32[768]{0:T(1024)}, u32[]{:S(2)}) copy-start(f32[768]{0:T(1024)} %param.26) | copy-start | bytes 9220
  114.6 75.4 %all-gather.11.cloned.1.call-start = ((), (), s32[]{:S(2)}) async-start(), calls=%async_computation.6 | async-start | bytes 4669440 | tf_op jit(solution)/shard_map/all_gather | solution.py:148
  153.3 3.4 copy-start
  156.6 4.7 copy-start.26
  158.2 75.7 %all-gather.21.cloned.1.call-start = ((), (), s32[]{:S(2)}) async-start(), calls=%async_computation.12 | async-start | bytes 1327104 | tf_op jit(solution)/shard_map/all_gather | solution.py:161
  158.7 107.0 %all-gather.19.cloned.1.call-start = ((), (), s32[]{:S(2)}) async-start(), calls=%async_computation.11 | async-start | bytes 4669440 | tf_op jit(solution)/shard_map/all_gather | solution.py:165
  161.4 148.1 %all-gather.13.cloned.1.call-start = ((), (), s32[]{:S(2)}) async-start(), calls=%async_computation.7 | async-start | bytes 1327104 | tf_op jit(solution)/shard_map/all_gather | solution.py:124
  162.1 189.7 %all-gather.15.cloned.1.call-start = ((), (), s32[]{:S(2)}) async-start(), calls=%async_computation.8 | async-start | bytes 1327104 | tf_op jit(solution)/shard_map/all_gather | solution.py:125
  162.9 102.9 %copy-start.35 = (f32[768]{0:T(1024)S(1)}, f32[768]{0:T(1024)}, u32[]{:S(2)}) copy-start(f32[768]{0:T(1024)} %param.28) | copy-start | bytes 9220
  162.9 212.1 %reduce-scatter.9.cloned.1.call-start = ((), (), s32[]{:S(2)}) async-start(), calls=%async_computation.13 | async-start | bytes 4669440 | tf_op jit(solution)/shard_map/reduce_scatter | solution.py:169
  292.7 122.4 %reduce-scatter.7.cloned.1.call-start = ((), (), s32[]{:S(2)}) async-start(), calls=%async_computation.9 | async-start | bytes 4669440 | tf_op jit(solution)/shard_map/reduce_scatter | solution.py:151
  374.8 2.1 copy-start.27
  374.8 40.3 %copy-start.23 = (f32[2,297]{1,0:T(2,128)S(1)}, f32[2,297]{1,0:T(2,128)}, u32[]{:S(2)}) copy-start(f32[2,297]{1,0:T(2,128)} %copy-done.22) | copy-start | bytes 7132
  374.9 40.3 %copy-start.31 = (f32[768]{0:T(1024)S(1)}, f32[768]{0:T(1024)}, u32[]{:S(2)}) copy-start(f32[768]{0:T(1024)} %param.30) | copy-start | bytes 9220
  374.9 132.4 %all-gather.23.cloned.1.call-start = ((), (), s32[]{:S(2)}) async-start(), calls=%async_computation.14 | async-start | bytes 4669440 | tf_op jit(solution)/shard_map/all_gather | solution.py:178
  374.9 2.0 copy-start.2
  377.9 40.9 %copy-start.14 = (bf16[192,96]{1,0:T(8,128)(2,1)S(1)}, bf16[192,96]{1,0:T(8,128)(2,1)}, u32[]{:S(2)}) copy-start(bf16[192,96]{1,0:T(8,128)(2,1)} %param.23) | copy-start | bytes 110596
  377.9 41.0 %copy-start.11 = (bf16[3,96,192]{2,1,0:T(8,128)(2,1)S(1)}, bf16[3,96,192]{2,1,0:T(8,128)(2,1)}, u32[]{:S(2)}) copy-start(bf16[3,96,192]{2,1,0:T(8,128)(2,1)} %param.22) | copy-start | bytes 331780
  418.7 155.6 %reduce-scatter.11.cloned.1.call-start = ((), (), s32[]{:S(2)}) async-start(), calls=%async_computation.15 | async-start | bytes 4669440 | tf_op jit(solution)/shard_map/reduce_scatter | solution.py:186
  489.3 7.7 %copy-start.7 = (bf16[3,768,192]{2,0,1:T(4,128)(2,1)}, bf16[3,768,192]{2,0,1:T(4,128)(2,1)S(1)}, u32[]{:S(2)}) copy-start(bf16[3,768,192]{2,0,1:T(4,128)(2,1)S(1)} %all_gather.47) | copy-start | bytes 2654212
  497.1 2.0 copy-start.33
  507.3 11.3 %slice-start = ((s8[11206656]{0:T(1024)(128)(4,1)}), s8[4194304]{0:T(1024)(128)(4,1)S(1)}, s32[]{:S(2)}) async-start(s8[11206656]{0:T(1024)(128)(4,1)} %bitcast.94), calls=%async_computation.17 | async-start | bytes 8388608
  510.9 7.7 %copy-start.37 = (bf16[8,297,192]{1,2,0:T(8,128)(2,1)}, bf16[8,297,192]{1,2,0:T(8,128)(2,1)S(1)}, u32[]{:S(2)}) copy-start(bf16[8,297,192]{1,2,0:T(8,128)(2,1)S(1)} %convolution_convert_fusion.1) | copy-start | bytes 2737156
  511.0 7.7 %slice-start.1 = ((s8[11206656]{0:T(1024)(128)(4,1)}), s8[4194304]{0:T(1024)(128)(4,1)S(1)}, s32[]{:S(2)}) async-start(s8[11206656]{0:T(1024)(128)(4,1)} %bitcast.94), calls=%async_computation.18 | async-start | bytes 8388608
  511.0 7.7 %slice-start.2 = ((s8[11206656]{0:T(1024)(128)(4,1)}), s8[2818048]{0:T(1024)(128)(4,1)S(1)}, s32[]{:S(2)}) async-start(s8[11206656]{0:T(1024)(128)(4,1)} %bitcast.94), calls=%async_computation.19 | async-start | bytes 5636096
  523.7 3.3 copy-start.5
  527.1 1.7 copy-start.36
  534.3 40.1 %copy-start.16 = (f32[2,297]{1,0:T(2,128)S(1)}, f32[2,297]{1,0:T(2,128)}, u32[]{:S(2)}) copy-start(f32[2,297]{1,0:T(2,128)} %copy-done.15) | copy-start | bytes 7132
  534.3 40.1 %copy-start.19 = (f32[768]{0:T(1024)S(1)}, f32[768]{0:T(1024)}, u32[]{:S(2)}) copy-start(f32[768]{0:T(1024)} %param.20) | copy-start | bytes 9220
  534.3 41.9 %copy-start.25 = (f32[2,297]{1,0:T(2,128)S(1)}, f32[2,297]{1,0:T(2,128)}, u32[]{:S(2)}) copy-start(f32[2,297]{1,0:T(2,128)} %copy-done.24) | copy-start | bytes 7132
  534.3 41.9 %copy-start.21 = (f32[2,297]{1,0:T(2,128)S(1)}, f32[2,297]{1,0:T(2,128)}, u32[]{:S(2)}) copy-start(f32[2,297]{1,0:T(2,128)} %copy-done.20) | copy-start | bytes 7132
  534.3 173.4 %all-reduce.2.cloned.1.call-start = ((), (), s32[]{:S(2)}) async-start(), calls=%async_computation.16 | async-start | bytes 638976 | tf_op jit(solution)/shard_map/psum | solution.py:191
  574.3 3.8 copy-start.1
  574.3 3.8 copy-start.3
  574.3 3.9 copy-start.4
  (6 other events, 8.3 us)
Sparse Core Ops, SparseCore 0:
  12.4 34.5 all-gather.8
  112.1 41.1 reduce-scatter.4
  292.9 41.6 reduce-scatter.8
  375.0 40.1 reduce-scatter.6
  582.0 125.6 all-reduce.1
Sparse Core Ops, SparseCore 1:
  114.8 41.0 all-gather.16
  158.2 31.7 all-gather.10
  192.3 41.5 all-gather.20
  235.5 30.2 all-gather.18
  268.0 41.5 all-gather.12
  311.7 40.0 all-gather.14
  418.8 31.7 all-gather.22
  534.4 39.9 reduce-scatter.10
where the time goes:
time: 726 us; the launch traced here: 717 us
  waiting for transfers between devices  371 us (51%)
  blocking collectives  142 us (20%)
  matrix products  132 us (18%)
  other arithmetic  26.4 us (4%)
  local copies, waits for them, and re-layouts  18.9 us (3%)
  between operations  16.4 us (2%)
  starting transfers between devices  9.95 us (1%)
    psum x1, waiting for transfers between devices, per_device(): lax.psum(jnp.sum(grad_stream[:, IMG_TOK:], axis=0), ('dp', 'head'))  120 us
    dot_general x4, matrix products, project(): jnp.einsum('isd,dc->isc', rows_b, weight, preferred_element_type=jnp.floa...  45.5 us
    all_gather x1, blocking collectives, per_device(): lax.all_gather(w_qkv, 'dp', axis=1, tiled=True)  40.5 us
    reduce_scatter x1, waiting for transfers between devices, per_device(): lax.psum_scatter(grad_partial.astype(jnp.bfloat16), 'head', scatter_dimen...  40 us
    all_gather x1, blocking collectives, per_device(): lax.all_gather(held_inputs[0], 'dp', axis=1, tiled=True)  39 us
    reduce_scatter x1, waiting for transfers between devices, per_device(): lax.psum_scatter(project(context, full_out).astype(jnp.bfloat16), 'head',...  38.6 us
    reduce_scatter x1, waiting for transfers between devices, per_device(): lax.psum_scatter(project(active_b, full_fc2).astype(jnp.bfloat16), 'head'...  37.2 us
    all_gather x1, waiting for transfers between devices, per_device(): lax.all_gather(held_inputs[3], 'dp', axis=1, tiled=True)  35.4 us
  transfers between devices with their start and end apart: 13, of which 9 were waited for; matrix products, arithmetic and copies ran while one was open for 15% of the time, Pallas kernels for 0%

commit v1 on v0

v1 whole, which is shorter than its diff:
```python
import functools

import jax
import jax.numpy as jnp
from jax import lax
from jax.experimental import pallas as pl
from jax.experimental.pallas import tpu as pltpu
from jax.sharding import PartitionSpec as P

HEAD_DIM = 64
IMG_TOK = 197
PROMPTS = 100
SEQ = IMG_TOK + PROMPTS
ROWS = 304
KEYS = 384
EPSILON = 1e-06
BOTH = ("dp", "head")
F32 = jnp.float32
BF16 = jnp.bfloat16

NN = (((1,), (0,)), ((), ()))
NT = (((1,), (1,)), ((), ()))
TN = (((0,), (0,)), ((), ()))


def dot(left, right, dims):
    return lax.dot_general(left, right, dims, preferred_element_type=F32)


def device_perm(count, target):
    pairs = []
    for index in range(count):
        c, y, x, z = index % 2, index // 2 % 2, index // 4 % 2, index // 8
        z, x, y, c = target(z, x, y, c)
        pairs.append((index, ((z * 2 + x) * 2 + y) * 2 + c))
    return pairs


class Exchange:
    def __init__(self, dp, head):
        self.count = dp * head
        self.depth = dp // 2

    def move(self, value, target):
        return lax.ppermute(value, BOTH, device_perm(self.count, target))

    def from_z(self, value, step):
        depth = self.depth
        return self.move(value, lambda z, x, y, c: ((z - step) % depth, x, y, c))

    def first(self, value):
        return self.move(value, lambda z, x, y, c: (z, x ^ (1 - c), y ^ c, c))

    def second(self, value):
        return self.move(value, lambda z, x, y, c: (z, x ^ c, y ^ (1 - c), c))

    def core(self, value):
        return self.move(value, lambda z, x, y, c: (z, x, y, 1 - c))

    def swap(self, value, dz=0, dx=0, dy=0):
        return self.move(value, lambda z, x, y, c: (z ^ dz, x ^ dx, y ^ dy, c))


def gather_pieces(exchange, piece, groups):
    arrived = {0: piece}
    for step in (1, 3, 2):
        arrived[step] = exchange.from_z(piece, step)
    arrays, plan = [], []
    for group in groups:
        base = jnp.stack([arrived[step] for step in group])
        near = jnp.concatenate([base, exchange.first(base)])
        far = exchange.second(near)
        for is_other, held in ((0, (near, far)), (1, (exchange.core(near), exchange.core(far)))):
            for is_far, array in enumerate(held):
                arrays.append(array)
                plan.append([(step, half, is_far, is_other) for half in (0, 1) for step in group])
    return arrays, plan


def placement(entry, place, depth):
    z, x, y, c = place
    step, half, is_far, is_other = entry
    core = c if not is_other else 1 - c
    moved_first, moved_second = half, is_far
    dx = jnp.where(core == 0, moved_first, moved_second)
    dy = jnp.where(core == 0, moved_second, moved_first)
    row = lax.rem(z + step, depth) * 2 + jnp.where(dx == 1, 1 - x, x)
    return dy * 2 + is_other, row


def load_weights(pieces, plan, place_ref, store, sems, depth):
    if plan is None:
        for slot in range(store.shape[0]):
            pltpu.make_async_copy(pieces[0].at[slot], store.at[slot], sems.at[slot]).start()
        return
    place = tuple(place_ref[i] for i in range(4))
    for ref, entries in zip(pieces, plan):
        for index, entry in enumerate(entries):
            slot, block = placement(entry, place, depth)
            rows = ref.shape[1]
            start = pl.multiple_of(block * rows, rows)
            pltpu.make_async_copy(
                ref.at[index], store.at[slot, pl.ds(start, rows)], sems.at[slot]
            ).start()


def wait_slot(store, sems, slot):
    pltpu.make_async_copy(store.at[slot], store.at[slot], sems.at[slot]).wait()


def row_mean(value):
    return jnp.mean(value, axis=-1, keepdims=True)


def normalized(rows):
    center = rows - row_mean(rows)
    scale = lax.rsqrt(row_mean(center * center) + EPSILON)
    return center * scale, scale


def norm_back(grad, gain, unit, scale):
    grad = grad * gain
    return scale * (grad - row_mean(grad) - unit * row_mean(grad * unit))


def low_lanes(shape):
    return lax.broadcasted_iota(jnp.int32, shape, len(shape) - 1) < HEAD_DIM


def half_of(tile, keep_low):
    keep = low_lanes(tile.shape)
    zero = jnp.zeros_like(tile)
    return jnp.where(keep, tile, zero) if keep_low else jnp.where(keep, zero, tile)


def attend_kernel(plan, depth, images, *refs):
    place, normed, stream, visible, b_out, gain, shift = refs[:7]
    count = 1 if plan is None else len(plan)
    pieces = refs[7 : 7 + count]
    qkv_out, probs_out, mid_out, normed_out, store, total, sems = refs[7 + count :]
    slot = pl.program_id(0)

    @pl.when(slot == 0)
    def _():
        load_weights(pieces, plan, place, store, sems, depth)
        total[...] = jnp.zeros_like(total)

    wait_slot(store, sems, slot)
    qkv = dot(normed[...], store[slot, :, :640], NN)
    for image in range(images):
        rows = slice(image * ROWS, (image + 1) * ROWS)
        qkv_out[0, image, :ROWS] = qkv[rows].astype(BF16)
        qkv_out[0, image, ROWS:] = jnp.zeros((KEYS - ROWS, 640), BF16)
    for image in range(images):
        rows = slice(image * ROWS, (image + 1) * ROWS)
        see = visible[image] > 0
        mixed = []
        for head in range(3):
            low = head != 1
            query_at, key_at, value_at = (0, 128, 256) if head < 2 else (384, 512, 384)
            query = half_of(qkv_out[0, image, :ROWS, query_at : query_at + 128], low)
            query = query * jnp.asarray(0.125, BF16)
            keys = qkv_out[0, image, :, key_at : key_at + 128]
            values = half_of(qkv_out[0, image, :, value_at : value_at + 128], head == 0)
            scores = jnp.where(see, dot(query, keys, NT), -1000000000.0)
            weight = jnp.exp(scores - jnp.max(scores, axis=-1, keepdims=True))
            probs = weight * (1.0 / jnp.sum(weight, axis=-1, keepdims=True))
            probs_b = probs.astype(BF16)
            probs_out[0, image * 3 + head] = probs_b
            mixed.append(dot(probs_b, values, NN))
        context = jnp.concatenate([mixed[2], mixed[0] + mixed[1]], axis=1).astype(BF16)
        total[rows] += dot(context, store[slot, :, 512:], NT)

    @pl.when(slot == pl.num_programs(0) - 1)
    def _():
        mid = stream[...].astype(F32) + total[...] + b_out[...]
        mid_out[...] = mid
        normed_out[...] = (normalized(mid)[0] * gain[...] + shift[...]).astype(BF16)


def gelu_parts(pre):
    density = jnp.exp(pre * pre * -0.5) * 0.3989422804014327
    chance = 0.5 + 0.5 * lax.erf(pre * 0.7071067811865476)
    return chance, density


def mlp_kernel(plan, depth, width, first, *refs):
    place, normed, grad, bias = refs[:4]
    refs = refs[4:]
    if not first:
        out_in, back_in = refs[:2]
        refs = refs[2:]
    count = 1 if plan is None else len(plan)
    pieces = refs[:count]
    out_sum, back_sum, store, sems = refs[count:]
    slot = pl.program_id(0)

    @pl.when(slot == 0)
    def _():
        load_weights(pieces, plan, place, store, sems, depth)
        if first:
            out_sum[...] = jnp.zeros_like(out_sum)
            back_sum[...] = jnp.zeros_like(back_sum)
        else:
            out_sum[...] = out_in[...]
            back_sum[...] = back_in[...]

    wait_slot(store, sems, slot)
    half = normed.shape[0] // 2
    for part in range(2):
        rows = slice(part * half, (part + 1) * half)
        pre = dot(normed[rows], store[slot, :, :width], NN) + bias[0]
        chance, density = gelu_parts(pre)
        active = (pre * chance).astype(BF16)
        slope = chance + pre * density
        out_sum[rows] += dot(active, store[slot, :, width:], NT)
        grad_active = dot(grad[rows], store[slot, :, width:], NN).astype(BF16).astype(F32)
        grad_pre = (grad_active * slope).astype(BF16)
        back_sum[rows] += dot(grad_pre, store[slot, :, :width], NT)


def back_kernel(plan, depth, images, *refs):
    place, lengths, mid, mlp_out, grad_normed, grad, stream, qkv, probs = refs[:9]
    gain_two, b_fc2, gain_one = refs[9:12]
    count = 1 if plan is None else len(plan)
    pieces = refs[12 : 12 + count]
    result, grad_input, grad_prompts, store, total, grad_mid, grad_attn, stacked, sems = refs[12 + count :]
    slot = pl.program_id(0)

    @pl.when(slot == 0)
    def _():
        load_weights(pieces, plan, place, store, sems, depth)
        total[...] = jnp.zeros_like(total)
        position = lax.broadcasted_iota(jnp.int32, (ROWS, 1), 0)
        for image in range(images):
            rows = slice(image * ROWS, (image + 1) * ROWS)
            used = (position < IMG_TOK + lengths[image]).astype(F32)
            rows_out = (mid[rows] + mlp_out[rows] + b_fc2[...]) * used
            result[image] = rows_out[:SEQ].astype(BF16)
            unit, scale = normalized(mid[rows])
            back = grad[rows].astype(F32) + norm_back(grad_normed[rows], gain_two[...], unit, scale)
            grad_mid[rows] = back
            grad_attn[rows] = back.astype(BF16)

    wait_slot(store, sems, slot)
    grad_context = dot(grad_attn[...], store[slot, :, 512:], NN).astype(BF16)
    for image in range(images):
        rows = slice(image * ROWS, (image + 1) * ROWS)
        tiles = {}

        def add(at, value):
            tiles[at] = value if at not in tiles else tiles[at] + value

        for head in range(3):
            low = head == 0
            grad_at = 128 if head < 2 else 0
            query_at, key_at, value_at = (0, 128, 256) if head < 2 else (384, 512, 384)
            grad_mix = half_of(grad_context[rows, grad_at : grad_at + 128], low)
            query = half_of(qkv[0, image, :ROWS, query_at : query_at + 128], head != 1)
            query = query * jnp.asarray(0.125, BF16)
            keys = half_of(qkv[0, image, :, key_at : key_at + 128], head != 1)
            keys = keys * jnp.asarray(0.125, BF16)
            values = qkv[0, image, :, value_at : value_at + 128]
            probs_b = probs[0, image * 3 + head]
            weight = probs_b.astype(F32)
            grad_probs = dot(grad_mix, values, NT)
            grad_scores = weight * (
                grad_probs - jnp.sum(weight * grad_probs, axis=-1, keepdims=True)
            )
            grad_scores = grad_scores.astype(BF16)
            add(value_at, dot(probs_b, grad_mix, TN)[:ROWS])
            add(query_at, dot(grad_scores, keys, NN))
            add(key_at, dot(grad_scores, query, TN)[:ROWS])
        for at, value in tiles.items():
            stacked[rows, at : at + 128] = value.astype(BF16)
    total[...] += dot(stacked[...], store[slot, :, :640], NT)

    @pl.when(slot == pl.num_programs(0) - 1)
    def _():
        prompt_sum = None
        for image in range(images):
            rows = slice(image * ROWS, (image + 1) * ROWS)
            unit, scale = normalized(stream[rows].astype(F32))
            back = grad_mid[rows] + norm_back(total[rows], gain_one[...], unit, scale)
            grad_input[image] = back[:IMG_TOK].astype(BF16)
            part = back[IMG_TOK:SEQ]
            prompt_sum = part if prompt_sum is None else prompt_sum + part
        grad_prompts[...] = prompt_sum


def whole(shape):
    return pl.BlockSpec(shape, lambda s: (0,) * len(shape))


ANY = pl.BlockSpec(memory_space=pl.ANY)
SMEM = pl.BlockSpec(memory_space=pltpu.SMEM)


def cost(flops, nbytes):
    return pl.CostEstimate(flops=int(flops), bytes_accessed=int(nbytes), transcendentals=0)


def attend(plan, depth, images, place, normed, stream, visible, b_out, gain, shift, pieces):
    rows, width = normed.shape
    slots = 4
    return pl.pallas_call(
        functools.partial(attend_kernel, plan, depth, images),
        grid=(slots,),
        in_specs=[
            SMEM,
            whole((rows, width)),
            whole((rows, width)),
            whole((images, 1, KEYS)),
            whole((1, width)),
            whole((1, width)),
            whole((1, width)),
        ]
        + [ANY] * len(pieces),
        out_specs=[
            pl.BlockSpec((1, images, KEYS, 640), lambda s: (s, 0, 0, 0)),
            pl.BlockSpec((1, images * 3, ROWS, KEYS), lambda s: (s, 0, 0, 0)),
            whole((rows, width)),
            whole((rows, width)),
        ],
        out_shape=[
            jax.ShapeDtypeStruct((slots, images, KEYS, 640), BF16),
            jax.ShapeDtypeStruct((slots, images * 3, ROWS, KEYS), BF16),
            jax.ShapeDtypeStruct((rows, width), F32),
            jax.ShapeDtypeStruct((rows, width), BF16),
        ],
        scratch_shapes=[
            pltpu.VMEM((slots, width, 768), BF16),
            pltpu.VMEM((rows, width), F32),
            pltpu.SemaphoreType.DMA((slots,)),
        ],
        compiler_params=pltpu.CompilerParams(vmem_limit_bytes=50 << 20),
        cost_estimate=cost(6e9, 1.6e7),
    )(place, normed, stream, visible, b_out, gain, shift, *pieces)


def mlp(plan, depth, place, normed, grad, bias, sums, pieces):
    rows, width = normed.shape
    slots, chunk = bias.shape[0], bias.shape[2]
    first = sums is None
    sums = () if first else tuple(sums)
    return pl.pallas_call(
        functools.partial(mlp_kernel, plan, depth, chunk, first),
        grid=(slots,),
        in_specs=[SMEM, whole((rows, width)), whole((rows, width))]
        + [pl.BlockSpec((1, 1, chunk), lambda s: (s, 0, 0))]
        + [whole((rows, width))] * len(sums)
        + [ANY] * len(pieces),
        out_specs=[whole((rows, width))] * 2,
        out_shape=[jax.ShapeDtypeStruct((rows, width), F32)] * 2,
        scratch_shapes=[
            pltpu.VMEM((slots, width, 2 * chunk), BF16),
            pltpu.SemaphoreType.DMA((slots,)),
        ],
        compiler_params=pltpu.CompilerParams(vmem_limit_bytes=50 << 20),
        cost_estimate=cost(8.0 * rows * width * chunk * slots, 1.6e7),
    )(place, normed, grad, bias, *sums, *pieces)


def attend_back(
    plan, depth, images, place, lengths, mid, mlp_out, grad_normed, grad, stream, qkv, probs,
    gain_two, b_fc2, gain_one, pieces,
):
    rows, width = mid.shape
    slots = 4
    row = whole((1, width))
    full = whole((rows, width))
    return pl.pallas_call(
        functools.partial(back_kernel, plan, depth, images),
        grid=(slots,),
        in_specs=[SMEM, SMEM, full, full, full, full, full]
        + [
            pl.BlockSpec((1, images, KEYS, 640), lambda s: (s, 0, 0, 0)),
            pl.BlockSpec((1, images * 3, ROWS, KEYS), lambda s: (s, 0, 0, 0)),
        ]
        + [row] * 3
        + [ANY] * len(pieces),
        out_specs=[
            whole((images, SEQ, width)),
            whole((images, IMG_TOK, width)),
            whole((PROMPTS, width)),
        ],
        out_shape=[
            jax.ShapeDtypeStruct((images, SEQ, width), BF16),
            jax.ShapeDtypeStruct((images, IMG_TOK, width), BF16),
            jax.ShapeDtypeStruct((PROMPTS, width), F32),
        ],
        scratch_shapes=[
            pltpu.VMEM((slots, width, 768), BF16),
            pltpu.VMEM((rows, width), F32),
            pltpu.VMEM((rows, width), F32),
            pltpu.VMEM((rows, width), BF16),
            pltpu.VMEM((rows, 640), BF16),
            pltpu.SemaphoreType.DMA((slots,)),
        ],
        compiler_params=pltpu.CompilerParams(vmem_limit_bytes=50 << 20),
        cost_estimate=cost(7e9, 2.4e7),
    )(
        place, lengths, mid, mlp_out, grad_normed, grad, stream, qkv, probs,
        gain_two, b_fc2, gain_one, *pieces,
    )


def layer_norm(rows, gain, shift):
    return normalized(rows)[0] * gain + shift


def sum_prompts(exchange, partial):
    half = partial.shape[1] // 2
    core = lax.axis_index("head") % 2
    low, high = partial[:, :half], partial[:, half:]
    keep = jnp.where(core == 0, low, high)
    give = jnp.where(core == 0, high, low)
    mine = keep + exchange.core(give.astype(BF16)).astype(F32)
    for move in ({"dx": 1}, {"dy": 1}, {"dz": 1}, {"dz": 2}):
        mine = lax.reduce_precision(mine, 8, 7)
        mine = mine + exchange.swap(mine.astype(BF16), **move).astype(F32)
    mine = lax.reduce_precision(mine, 8, 7)
    other = exchange.core(mine.astype(BF16)).astype(F32)
    return jnp.where(
        core == 0,
        jnp.concatenate([mine, other], axis=1),
        jnp.concatenate([other, mine], axis=1),
    )


def per_device(
    exchange,
    layer_input,
    prompts,
    lengths,
    key_mask,
    ln1_gain,
    ln1_shift,
    w_qkv,
    w_out,
    b_out,
    ln2_gain,
    ln2_shift,
    w_fc1,
    b_fc1,
    w_fc2,
    b_fc2,
    grad_output,
):
    images, _, width = layer_input.shape
    chunks = (256, 512)

    out_t, fc2_t = w_out.T, w_fc2.T
    query, key, value = w_qkv[0], w_qkv[1], w_qkv[2]
    piece_attn = jnp.concatenate(
        [query[:, :128], key[:, :128], value[:, :128], query[:, 128:], value[:, 128:]]
        + [key[:, 128:], out_t[:, 128:], out_t[:, :128]],
        axis=1,
    )
    pieces_mlp, start = [], 0
    for chunk in chunks:
        pieces_mlp.append(
            jnp.concatenate(
                [w_fc1[:, start : start + chunk], fc2_t[:, start : start + chunk]], axis=1
            )
        )
        start += chunk

    if exchange is not None:
        depth = exchange.depth
        dp, head = lax.axis_index("dp"), lax.axis_index("head")
        place = jnp.stack([dp // 2, dp % 2, head // 2, head % 2]).astype(jnp.int32)
        attn, plan_attn = gather_pieces(exchange, piece_attn, ((0,), (1, 3, 2)))
        gathered = [gather_pieces(exchange, piece, ((0,), (1, 3, 2))) for piece in pieces_mlp]
        bias = jnp.stack([b_fc1, exchange.core(b_fc1)])
        bias = jnp.concatenate([bias, exchange.swap(bias, dy=1)])
    else:
        depth = 0
        place = jnp.zeros((4,), jnp.int32)

        def gather_whole(piece):
            rows = lax.all_gather(piece, "dp", axis=0, tiled=True)
            return [lax.all_gather(rows, "head", axis=0)], None

        attn, plan_attn = gather_whole(piece_attn)
        gathered = [gather_whole(piece) for piece in pieces_mlp]
        bias = lax.all_gather(b_fc1, "head", axis=0)

    own_at = lax.axis_index("head") * images
    own_lengths = lax.dynamic_slice_in_dim(lengths, own_at, images, 0)
    own_mask = lax.dynamic_slice_in_dim(key_mask, own_at, images, 0)
    position = lax.broadcasted_iota(jnp.int32, (images, SEQ), 1)
    used = (position < IMG_TOK) | (position - IMG_TOK < own_lengths[:, None])
    visible = used & ((own_mask == 1) | (position == 0))
    visible = jnp.pad(visible.astype(F32), ((0, 0), (0, KEYS - SEQ)))[:, None, :]
    prompt_rows = jnp.broadcast_to(prompts[None], (images, PROMPTS, width))
    padding = jnp.zeros((images, ROWS - SEQ, width), BF16)
    stream = jnp.concatenate([layer_input, prompt_rows, padding], axis=1)
    stream = stream.reshape(images * ROWS, width)
    grad = jnp.where(used[:, :, None], grad_output, jnp.zeros_like(grad_output))
    grad = jnp.concatenate([grad, padding], axis=1).reshape(images * ROWS, width)
    normed = layer_norm(stream.astype(F32), ln1_gain, ln1_shift).astype(BF16)

    row = lambda vector: vector.reshape(1, width)
    qkv, probs, mid, normed_mlp = attend(
        plan_attn, depth, images, place, normed, stream, visible,
        row(b_out), row(ln2_gain), row(ln2_shift), attn,
    )
    sums, start = None, 0
    for chunk, (pieces, plan) in zip(chunks, gathered):
        chunk_bias = bias[:, None, start : start + chunk]
        sums = mlp(plan, depth, place, normed_mlp, grad, chunk_bias, sums, pieces)
        start += chunk
    result, grad_input, partial = attend_back(
        plan_attn, depth, images, place, own_lengths, mid, sums[0], sums[1], grad, stream,
        qkv, probs, row(ln2_gain), row(b_fc2), row(ln1_gain), attn,
    )
    if exchange is not None:
        grad_prompts = sum_prompts(exchange, partial)
    else:
        grad_prompts = lax.psum(partial, BOTH)
    return (result, grad_input, grad_prompts)


def solution(mesh):
    dp, head = mesh.shape["dp"], mesh.shape["head"]
    exchange = Exchange(dp, head) if (dp, head) == (8, 4) else None
    placed = (
        P(BOTH, None, None),
        P(),
        P("dp"),
        P("dp", None),
        P(),
        P(),
        P(None, "dp", "head"),
        P("head", "dp"),
        P(),
        P(),
        P(),
        P("dp", "head"),
        P("head"),
        P("head", "dp"),
        P(),
        P(BOTH, None, None),
    )
    return jax.shard_map(
        functools.partial(per_device, exchange),
        mesh=mesh,
        in_specs=placed,
        out_specs=(P(BOTH, None, None), P(BOTH, None, None), P()),
        check_vma=False,
    )
```

time: 726 us -> 226 us (0.31); the launches traced: 717 us -> 225 us
  waiting for transfers between devices: 371 us -> 66.7 us
  blocking collectives: 142 us -> 0 us
  matrix products: 132 us -> 0 us
  Pallas kernels: 0 us -> 82.5 us
  starting transfers between devices: 9.95 us -> 37.6 us
  between operations: 16.4 us -> 1.28 us
  other arithmetic: 26.4 us -> 18.2 us
    all_gather x4 -> x0, blocking collectives: 142 us -> none  [the longest x1 40.5 us: per_device(): lax.all_gather(w_qkv, 'dp', axis=1, tiled=True)]
    all_gather x8 -> x0, waiting for transfers between devices: 133 us -> none  [the longest x1 35.4 us: per_device(): lax.all_gather(held_inputs[3], 'dp', axis=1, tiled=True)]
    psum x1 -> x0, waiting for transfers between devices: 120 us -> none  [per_device(): lax.psum(jnp.sum(grad_stream[:, IMG_TOK:], axis=0), ('dp', 'head'))]
    dot_general x14 -> x0, matrix products: 116 us -> none  [the longest x4 45.5 us: project(): jnp.einsum('isd,dc->isc', rows_b, weight, preferred_element_type=jnp.floa...]
    reduce_scatter x4 -> x0, waiting for transfers between devices: 116 us -> none  [the longest x1 40 us: per_device(): lax.psum_scatter(grad_partial.astype(jnp.bfloat16), 'head', scatter_dimen...]
    pallas_call x0 -> x4, Pallas kernels: none -> 82.5 us  [the longest x1 30.6 us: attend_back(): pl.pallas_call(functools.partial(back_kernel, plan, depth, images), grid=...]
    ppermute x0 -> x41, waiting for transfers between devices: none -> 66.7 us  [move(): return lax.ppermute(value, BOTH, device_perm(self.count, target))]
    ppermute x0 -> x41, starting transfers between devices: none -> 37.6 us  [move(): return lax.ppermute(value, BOTH, device_perm(self.count, target))]
  transfers between devices with their start and end apart: 13 -> 41, of which waited for: 9 -> 12; matrix products, arithmetic and copies ran while one was open for 15% -> 14% of each run, Pallas kernels for 0% -> 16%
where the time goes in v1:
time: 226 us; the launch traced here: 225 us
  Pallas kernels  82.5 us (37%)
  waiting for transfers between devices  66.7 us (30%)
  starting transfers between devices  37.6 us (17%)
  local copies, waits for them, and re-layouts  18.6 us (8%)
  other arithmetic  18.2 us (8%)
    ppermute x41, waiting for transfers between devices, move(): return lax.ppermute(value, BOTH, device_perm(self.count, target))  66.7 us
    ppermute x41, starting transfers between devices, move(): return lax.ppermute(value, BOTH, device_perm(self.count, target))  37.6 us
    pallas_call x1, Pallas kernels, attend_back(): pl.pallas_call(functools.partial(back_kernel, plan, depth, images), grid=...  30.6 us
    pallas_call x2, Pallas kernels, mlp(): pl.pallas_call(functools.partial(mlp_kernel, plan, depth, chunk, first),...  28.8 us
    pallas_call x1, Pallas kernels, attend(): pl.pallas_call(functools.partial(attend_kernel, plan, depth, images), gri...  23 us
    unnamed x52, local copies, waits for them, and re-layouts  7.94 us
    reduce_sum x2, other arithmetic, row_mean(): return jnp.mean(value, axis=-1, keepdims=True)  5.92 us
  transfers between devices with their start and end apart: 41, of which 12 were waited for; matrix products, arithmetic and copies ran while one was open for 14% of the time, Pallas kernels for 16%

profile of v1, /device:TPU:0, one launch (start us, length us, event | category | flops | bytes accessed | tf_op | source)
XLA Modules:
  0.0 224.8 jit_solution(18206081110493201527)
XLA Ops:
  0.7 0.9 slice_bitcast_fusion
  2.7 5.1 %collective-permute-start.4 = (bf16[96,768]{1,0:T(8,128)(2,1)S(1)}, bf16[96,768]{1,0:T(8,128)(2,1)S(1)}, u32[]{:S(2)}, u32[]{:S(2)}) collective-permute-start(bf16[96,768]{1,0:T(8,128)(2,1)S(1)} %concatenate.47), channel_id=1, source_target_pairs={{0,24},{1,25},{2,26},{3,27},{4,28},{5,29},{6,30},{7,31},{8,0},{9,1... | collective-permute-start | bytes 442376 | tf_op jit(solution)/shard_map/ppermute | solution.py:45
  7.8 1.0 collective-permute-start.6
  10.6 2.9 %collective-permute-start.28 = (bf16[96,1024]{1,0:T(8,128)(2,1)S(1)}, bf16[96,1024]{1,0:T(8,128)(2,1)S(1)}, u32[]{:S(2)}, u32[]{:S(2)}) collective-permute-start(bf16[96,1024]{1,0:T(8,128)(2,1)S(1)} %get-tuple-element.45), channel_id=1, source_target_pairs={{0,24},{1,25},{2,26},{3,27},{4,28},{5,29},{6,30},{7,31},{8,0},{9,1... | collective-permute-start | bytes 589832 | tf_op jit(solution)/shard_map/ppermute | solution.py:45
  13.8 4.1 %convert_reduce_fusion = (f32[2,304]{0,1:T(8,128)S(1)}, bf16[2,304,768]{2,0,1:T(2,128)(2,1)S(1)}) fusion(bf16[304]{0:T(512)(128)(2,1)S(1)} %pad.49.clone, bf16[2,100,768]{2,0,1:T(2,128)(2,1)S(1)} %broadcast_in_dim.39, bf16[2,197,768]{2,0,1:T(2,128)(2,1)S(1)} %copy-done.10), kind=kLoop, calls=%fused_computation.1 | loop fusion | flops 1867168 | bytes 1849312 | tf_op jit(solution)/shard_map/reduce_sum | solution.py:112
  17.9 1.9 fusion.1
  20.6 1.1 copy.43
  22.7 1.5 collective-permute-start.30
  24.3 3.0 %collective-permute-start.17 = (bf16[96,512]{1,0:T(8,128)(2,1)S(1)}, bf16[96,512]{1,0:T(8,128)(2,1)S(1)}, u32[]{:S(2)}, u32[]{:S(2)}) collective-permute-start(bf16[96,512]{1,0:T(8,128)(2,1)S(1)} %get-tuple-element.50), channel_id=1, source_target_pairs={{0,24},{1,25},{2,26},{3,27},{4,28},{5,29},{6,30},{7,31},{8,0},{9,1... | collective-permute-start | bytes 294920 | tf_op jit(solution)/shard_map/ppermute | solution.py:45
  27.3 1.0 collective-permute-start.19
  28.3 3.5 %collective-permute-done.29 = bf16[96,1024]{1,0:T(8,128)(2,1)S(1)} collective-permute-done((bf16[96,1024]{1,0:T(8,128)(2,1)S(1)}, bf16[96,1024]{1,0:T(8,128)(2,1)S(1)}, u32[]{:S(2)}, u32[]{:S(2)}) %collective-permute-start.29) | collective-permute-done | bytes 196640 | tf_op jit(solution)/shard_map/ppermute | solution.py:45
  31.8 1.5 collective-permute-start.13
  33.3 10.4 %collective-permute-done.30 = bf16[96,1024]{1,0:T(8,128)(2,1)S(1)} collective-permute-done((bf16[96,1024]{1,0:T(8,128)(2,1)S(1)}, bf16[96,1024]{1,0:T(8,128)(2,1)S(1)}, u32[]{:S(2)}, u32[]{:S(2)}) %collective-permute-start.30) | collective-permute-done | bytes 196640 | tf_op jit(solution)/shard_map/ppermute | solution.py:45
  43.8 1.5 collective-permute-start.7
  45.9 1.5 collective-permute-start.31
  48.1 1.5 collective-permute-start.14
  49.7 6.1 %collective-permute-done = bf16[1,96,768]{2,1,0:T(8,128)(2,1)S(1)} collective-permute-done((bf16[1,96,768]{2,1,0:T(8,128)(2,1)S(1)}, bf16[1,96,768]{2,1,0:T(8,128)(2,1)S(1)}, u32[]{:S(2)}, u32[]{:S(2)}) %collective-permute-start) | collective-permute-done | bytes 147488 | tf_op jit(solution)/shard_map/ppermute | solution.py:45
  55.8 1.6 collective-permute-start.20
  57.5 6.7 %collective-permute-done.24 = bf16[1,96,1024]{2,1,0:T(8,128)(2,1)S(1)} collective-permute-done((bf16[1,96,1024]{2,1,0:T(8,128)(2,1)S(1)}, bf16[1,96,1024]{2,1,0:T(8,128)(2,1)S(1)}, u32[]{:S(2)}, u32[]{:S(2)}) %collective-permute-start.24) | collective-permute-done | bytes 196640 | tf_op jit(solution)/shard_map/ppermute | solution.py:45
  64.2 1.5 collective-permute-start.8
  66.3 1.2 pad_maximum_fusion.refs_10_
  67.5 9.9 %collective-permute-done.12 = f32[2,768]{1,0:T(2,128)} collective-permute-done((f32[2,768]{1,0:T(2,128)S(1)}, f32[2,768]{1,0:T(2,128)}, u32[]{:S(2)}, u32[]{:S(2)}) %collective-permute-start.12) | collective-permute-done | bytes 6176 | tf_op jit(solution)/shard_map/ppermute | solution.py:45
  77.4 1.5 collective-permute-start.1
  79.5 1.5 collective-permute-start.32
  81.0 1.4 add_convert_fusion.refs_1_
  82.5 1.6 collective-permute-done.1.refs_8_.refs_13_
  85.3 1.1 pad_maximum_fusion.2.refs_8_
  87.2 1.5 collective-permute-start.21
  89.2 1.3 or_and_fusion
  91.4 1.3 pad_convert_fusion
  92.7 3.0 %broadcast_select_fusion = bf16[2,297,768]{2,0,1:T(2,128)(2,1)} fusion(bf16[2,297,768]{2,0,1:T(2,128)(2,1)} %param.31, pred[2,297]{0,1:T(8,128)(4,1)} %copy.48), kind=kLoop, calls=%fused_computation.5 | loop fusion | flops 456192 | bytes 1825362 | tf_op jit(solution)/shard_map/jit(_where)/select_n | solution.py:500
  95.7 11.7 %collective-permute-done.21.refs_9_ = bf16[6,96,512]{2,1,0:T(8,128)(2,1)} collective-permute-done((bf16[6,96,512]{2,1,0:T(8,128)(2,1)S(1)}, bf16[6,96,512]{2,1,0:T(8,128)(2,1)}, u32[]{:S(2)}, u32[]{:S(2)}) %collective-permute-start.21) | collective-permute-done | bytes 589856 | tf_op jit(solution)/shard_map/ppermute | solution.py:45
  111.4 1.3 copy.53
  112.8 1.1 concatenate.50.clone
  116.0 23.0 %shard_map.175 = (bf16[4,2,384,640]{3,2,1,0:T(8,128)(2,1)}, bf16[4,6,304,384]{3,2,1,0:T(8,128)(2,1)}, f32[608,768]{1,0:T(8,128)}, bf16[608,768]{1,0:T(8,128)(2,1)}) custom-call(s32[4]{0:T(128)S(1)} %pad_add_fusion.refs_0_, bf16[608,768]{1,0:T(8,128)(2,1)} %add_convert_fusion.refs_1_, bf16[608,768]{1,0:T(8,128)(2,1)} %bitcast.34, ...), custom_call_target="tpu_custom_call" | custom-call | flops 6000000000 | bytes 16000000 | tf_op jit(solution)/shard_map/pallas_call | solution.py:306
  139.1 1.2 copy-done.7
  140.3 12.0 %shard_map.176 = (f32[608,768]{1,0:T(8,128)}, f32[608,768]{1,0:T(8,128)}) custom-call(s32[4]{0:T(128)S(1)} %pad_add_fusion.refs_0_, bf16[608,768]{1,0:T(8,128)(2,1)S(1)} %copy-done.7, bf16[608,768]{1,0:T(8,128)(2,1)} %bitcast.31, f32[4,1,256]{2,1,0:T(1,128)S(1)} %copy.50.refs_3_, bf16[2,96,512]{2,1,0:T(8,128)(2,1)S(1)} %pad_maximum_fusion.8.refs_4_, ...), custom_call_target="tpu_custom_call" | custom-call | flops 3825205248 | bytes 16000000 | tf_op jit(solution)/shard_map/pallas_call | solution.py:346
  152.3 16.9 %shard_map.177 = (f32[608,768]{1,0:T(8,128)}, f32[608,768]{1,0:T(8,128)}) custom-call(s32[4]{0:T(128)S(1)} %pad_add_fusion.refs_0_, bf16[608,768]{1,0:T(8,128)(2,1)S(1)} %copy-done.7, bf16[608,768]{1,0:T(8,128)(2,1)S(1)} %bitcast.33, f32[4,1,512]{2,1,0:T(1,128)S(1)} %broadcast_in_dim.45.refs_3_, f32[608,768]{1,0:T(8,128)} %get-tuple-element.16.refs_4_, ...), custom_call_target="tpu_custom_call" | custom-call | flops 7650410496 | bytes 16000000 | tf_op jit(solution)/shard_map/pallas_call | solution.py:346
  169.2 30.6 %shard_map.178 = (bf16[2,297,768]{2,1,0:T(8,128)(2,1)}, bf16[2,197,768]{2,1,0:T(8,128)(2,1)S(1)}, f32[100,768]{1,0:T(8,128)S(1)}) custom-call(s32[4]{0:T(128)S(1)} %pad_add_fusion.refs_0_, s32[2]{0:T(128)S(1)} %dynamic_slice.6.refs_1_, f32[608,768]{1,0:T(8,128)} %get-tuple-element.14.refs_2_, f32[608,768]{1,0:T(8,128)} %get-tuple-element.18.refs_3_, ...), custom_call_target="tpu_custom_call" | custom-call | flops 7000000000 | bytes 24000000 | tf_op jit(solution)/shard_map/pallas_call | solution.py:372
  200.5 0.9 collective-permute-done.35
  201.4 1.6 collective-permute-start.36
  203.0 3.2 %collective-permute-done.36 = bf16[100,384]{1,0:T(8,128)(2,1)S(1)} collective-permute-done((bf16[100,384]{1,0:T(8,128)(2,1)S(1)}, bf16[100,384]{1,0:T(8,128)(2,1)S(1)}, u32[]{:S(2)}, u32[]{:S(2)}) %collective-permute-start.36) | collective-permute-done | bytes 76832 | tf_op jit(solution)/shard_map/ppermute | solution.py:45
  206.2 1.6 collective-permute-start.37
  207.8 2.9 %collective-permute-done.37 = bf16[100,384]{1,0:T(8,128)(2,1)S(1)} collective-permute-done((bf16[100,384]{1,0:T(8,128)(2,1)S(1)}, bf16[100,384]{1,0:T(8,128)(2,1)S(1)}, u32[]{:S(2)}, u32[]{:S(2)}) %collective-permute-start.37) | collective-permute-done | bytes 76832 | tf_op jit(solution)/shard_map/ppermute | solution.py:45
  210.8 4.4 %collective-permute-done.38 = bf16[100,384]{1,0:T(8,128)(2,1)S(1)} collective-permute-done((bf16[100,384]{1,0:T(8,128)(2,1)S(1)}, bf16[100,384]{1,0:T(8,128)(2,1)S(1)}, u32[]{:S(2)}, u32[]{:S(2)}) %collective-permute-start.38) | collective-permute-done | bytes 76832 | tf_op jit(solution)/shard_map/ppermute | solution.py:45
  215.6 5.4 %collective-permute-done.39 = bf16[100,384]{1,0:T(8,128)(2,1)S(1)} collective-permute-done((bf16[100,384]{1,0:T(8,128)(2,1)S(1)}, bf16[100,384]{1,0:T(8,128)(2,1)S(1)}, u32[]{:S(2)}, u32[]{:S(2)}) %collective-permute-start.39) | collective-permute-done | bytes 76832 | tf_op jit(solution)/shard_map/ppermute | solution.py:45
  221.1 1.6 copy.51
  222.8 1.3 copy.52
  (158 shorter events, 19.4 us)
Async XLA Ops:
  2.7 20.0 %collective-permute-start.4 = (bf16[96,768]{1,0:T(8,128)(2,1)S(1)}, bf16[96,768]{1,0:T(8,128)(2,1)S(1)}, u32[]{:S(2)}, u32[]{:S(2)}) collective-permute-start(bf16[96,768]{1,0:T(8,128)(2,1)S(1)} %concatenate.47), channel_id=1, source_target_pairs={{0,24},{1,25},{2,26},{3,27},{4,28},{5,29},{6,30},{7,31},{8,0},{9,1... | collective-permute-start | bytes 442376 | tf_op jit(solution)/shard_map/ppermute | solution.py:45
  7.8 16.5 %collective-permute-start.5 = (bf16[96,768]{1,0:T(8,128)(2,1)S(1)}, bf16[96,768]{1,0:T(8,128)(2,1)S(1)}, u32[]{:S(2)}, u32[]{:S(2)}) collective-permute-start(bf16[96,768]{1,0:T(8,128)(2,1)S(1)} %concatenate.47), channel_id=1, source_target_pairs={{0,8},{1,9},{2,10},{3,11},{4,12},{5,13},{6,14},{7,15},{8,16},{9,17... | collective-permute-start | bytes 442376 | tf_op jit(solution)/shard_map/ppermute | solution.py:45
  7.8 19.5 %collective-permute-start.6 = (bf16[96,768]{1,0:T(8,128)(2,1)S(1)}, bf16[96,768]{1,0:T(8,128)(2,1)S(1)}, u32[]{:S(2)}, u32[]{:S(2)}) collective-permute-start(bf16[96,768]{1,0:T(8,128)(2,1)S(1)} %concatenate.47), channel_id=1, source_target_pairs={{0,16},{1,17},{2,18},{3,19},{4,20},{5,21},{6,22},{7,23},{8,24},{9,... | collective-permute-start | bytes 442376 | tf_op jit(solution)/shard_map/ppermute | solution.py:45
  8.8 13.3 %collective-permute-start.11 = (f32[768]{0:T(1024)}, f32[768]{0:T(1024)S(1)}, u32[]{:S(2)}, u32[]{:S(2)}) collective-permute-start(f32[768]{0:T(1024)} %param.28), channel_id=1, source_target_pairs={{0,1},{1,0},{2,3},{3,2},{4,5},{5,4},{6,7},{7,6},{8,9},{9,8},{10,11... | collective-permute-start | bytes 9224 | tf_op jit(solution)/shard_map/ppermute | solution.py:45
  10.6 16.7 %collective-permute-start.28 = (bf16[96,1024]{1,0:T(8,128)(2,1)S(1)}, bf16[96,1024]{1,0:T(8,128)(2,1)S(1)}, u32[]{:S(2)}, u32[]{:S(2)}) collective-permute-start(bf16[96,1024]{1,0:T(8,128)(2,1)S(1)} %get-tuple-element.45), channel_id=1, source_target_pairs={{0,24},{1,25},{2,26},{3,27},{4,28},{5,29},{6,30},{7,31},{8,0},{9,1... | collective-permute-start | bytes 589832 | tf_op jit(solution)/shard_map/ppermute | solution.py:45
  22.1 9.7 %collective-permute-start.29 = (bf16[96,1024]{1,0:T(8,128)(2,1)S(1)}, bf16[96,1024]{1,0:T(8,128)(2,1)S(1)}, u32[]{:S(2)}, u32[]{:S(2)}) collective-permute-start(bf16[96,1024]{1,0:T(8,128)(2,1)S(1)} %get-tuple-element.45), channel_id=1, source_target_pairs={{0,8},{1,9},{2,10},{3,11},{4,12},{5,13},{6,14},{7,15},{8,16},{9,17... | collective-permute-start | bytes 589832 | tf_op jit(solution)/shard_map/ppermute | solution.py:45
  22.7 34.7 %copy-start.16 = (f32[1,768]{1,0:T(1,128)}, f32[1,768]{1,0:T(1,128)S(1)}, u32[]{:S(2)}) copy-start(f32[1,768]{1,0:T(1,128)S(1)} %stack.80) | copy-start | bytes 9220
  22.7 21.0 %collective-permute-start.30 = (bf16[96,1024]{1,0:T(8,128)(2,1)S(1)}, bf16[96,1024]{1,0:T(8,128)(2,1)S(1)}, u32[]{:S(2)}, u32[]{:S(2)}) collective-permute-start(bf16[96,1024]{1,0:T(8,128)(2,1)S(1)} %get-tuple-element.45), channel_id=1, source_target_pairs={{0,16},{1,17},{2,18},{3,19},{4,20},{5,21},{6,22},{7,23},{8,24},{9,... | collective-permute-start | bytes 589832 | tf_op jit(solution)/shard_map/ppermute | solution.py:45
  24.3 21.0 %collective-permute-start.17 = (bf16[96,512]{1,0:T(8,128)(2,1)S(1)}, bf16[96,512]{1,0:T(8,128)(2,1)S(1)}, u32[]{:S(2)}, u32[]{:S(2)}) collective-permute-start(bf16[96,512]{1,0:T(8,128)(2,1)S(1)} %get-tuple-element.50), channel_id=1, source_target_pairs={{0,24},{1,25},{2,26},{3,27},{4,28},{5,29},{6,30},{7,31},{8,0},{9,1... | collective-permute-start | bytes 294920 | tf_op jit(solution)/shard_map/ppermute | solution.py:45
  27.2 20.2 %collective-permute-start.18 = (bf16[96,512]{1,0:T(8,128)(2,1)S(1)}, bf16[96,512]{1,0:T(8,128)(2,1)S(1)}, u32[]{:S(2)}, u32[]{:S(2)}) collective-permute-start(bf16[96,512]{1,0:T(8,128)(2,1)S(1)} %get-tuple-element.50), channel_id=1, source_target_pairs={{0,8},{1,9},{2,10},{3,11},{4,12},{5,13},{6,14},{7,15},{8,16},{9,17... | collective-permute-start | bytes 294920 | tf_op jit(solution)/shard_map/ppermute | solution.py:45
  27.3 20.8 %collective-permute-start.19 = (bf16[96,512]{1,0:T(8,128)(2,1)S(1)}, bf16[96,512]{1,0:T(8,128)(2,1)S(1)}, u32[]{:S(2)}, u32[]{:S(2)}) collective-permute-start(bf16[96,512]{1,0:T(8,128)(2,1)S(1)} %get-tuple-element.50), channel_id=1, source_target_pairs={{0,16},{1,17},{2,18},{3,19},{4,20},{5,21},{6,22},{7,23},{8,24},{9,... | collective-permute-start | bytes 294920 | tf_op jit(solution)/shard_map/ppermute | solution.py:45
  31.8 14.1 %collective-permute-start.13 = (bf16[1,96,512]{2,1,0:T(8,128)(2,1)S(1)}, bf16[1,96,512]{2,1,0:T(8,128)(2,1)S(1)}, u32[]{:S(2)}, u32[]{:S(2)}) collective-permute-start(bf16[1,96,512]{2,1,0:T(8,128)(2,1)S(1)} %get-tuple-element.51), channel_id=1, source_target_pairs={{0,4},{1,3},{2,6},{3,1},{4,0},{5,7},{6,2},{7,5},{8,12},{9,11},{10,... | collective-permute-start | bytes 294920 | tf_op jit(solution)/shard_map/ppermute | solution.py:45
  43.8 12.0 %collective-permute-start.7 = (bf16[3,96,768]{2,1,0:T(8,128)(2,1)S(1)}, bf16[3,96,768]{2,1,0:T(8,128)(2,1)S(1)}, u32[]{:S(2)}, u32[]{:S(2)}) collective-permute-start(bf16[3,96,768]{2,1,0:T(8,128)(2,1)S(1)} %pad_maximum_fusion.4), channel_id=1, source_target_pairs={{0,4},{1,3},{2,6},{3,1},{4,0},{5,7},{6,2},{7,5},{8,12},{9,11},{10,... | collective-permute-start | bytes 1327112 | tf_op jit(solution)/shard_map/ppermute | solution.py:45
  45.3 10.4 %collective-permute-start = (bf16[1,96,768]{2,1,0:T(8,128)(2,1)S(1)}, bf16[1,96,768]{2,1,0:T(8,128)(2,1)S(1)}, u32[]{:S(2)}, u32[]{:S(2)}) collective-permute-start(bf16[1,96,768]{2,1,0:T(8,128)(2,1)S(1)} %bitcast.48), channel_id=1, source_target_pairs={{0,4},{1,3},{2,6},{3,1},{4,0},{5,7},{6,2},{7,5},{8,12},{9,11},{10,... | collective-permute-start | bytes 442376 | tf_op jit(solution)/shard_map/ppermute | solution.py:45
  45.9 19.8 %collective-permute-start.31 = (bf16[3,96,1024]{2,1,0:T(8,128)(2,1)S(1)}, bf16[3,96,1024]{2,1,0:T(8,128)(2,1)S(1)}, u32[]{:S(2)}, u32[]{:S(2)}) collective-permute-start(bf16[3,96,1024]{2,1,0:T(8,128)(2,1)S(1)} %pad_maximum_fusion.3), channel_id=1, source_target_pairs={{0,4},{1,3},{2,6},{3,1},{4,0},{5,7},{6,2},{7,5},{8,12},{9,11},{10,... | collective-permute-start | bytes 1769480 | tf_op jit(solution)/shard_map/ppermute | solution.py:45
  47.5 16.7 %collective-permute-start.24 = (bf16[1,96,1024]{2,1,0:T(8,128)(2,1)S(1)}, bf16[1,96,1024]{2,1,0:T(8,128)(2,1)S(1)}, u32[]{:S(2)}, u32[]{:S(2)}) collective-permute-start(bf16[1,96,1024]{2,1,0:T(8,128)(2,1)S(1)} %get-tuple-element.46), channel_id=1, source_target_pairs={{0,4},{1,3},{2,6},{3,1},{4,0},{5,7},{6,2},{7,5},{8,12},{9,11},{10,... | collective-permute-start | bytes 589832 | tf_op jit(solution)/shard_map/ppermute | solution.py:45
  48.1 30.8 %collective-permute-start.14 = (bf16[2,96,512]{2,1,0:T(8,128)(2,1)S(1)}, bf16[2,96,512]{2,1,0:T(8,128)(2,1)}, u32[]{:S(2)}, u32[]{:S(2)}) collective-permute-start(bf16[2,96,512]{2,1,0:T(8,128)(2,1)S(1)} %pad_maximum_fusion.8.refs_4_), channel_id=1, source_target_pairs={{0,2},{1,5},{2,0},{3,7},{4,6},{5,1},{6,4},{7,3},{8,10},{9,13},{10,... | collective-permute-start | bytes 589832 | tf_op jit(solution)/shard_map/ppermute | solution.py:45
  55.7 23.2 %collective-permute-start.15 = (bf16[2,96,512]{2,1,0:T(8,128)(2,1)S(1)}, bf16[2,96,512]{2,1,0:T(8,128)(2,1)S(1)}, u32[]{:S(2)}, u32[]{:S(2)}) collective-permute-start(bf16[2,96,512]{2,1,0:T(8,128)(2,1)S(1)} %pad_maximum_fusion.8.refs_4_), channel_id=1, source_target_pairs={{0,1},{1,0},{2,3},{3,2},{4,5},{5,4},{6,7},{7,6},{8,9},{9,8},{10,11... | collective-permute-start | bytes 589832 | tf_op jit(solution)/shard_map/ppermute | solution.py:45
  55.8 23.7 %collective-permute-start.20 = (bf16[3,96,512]{2,1,0:T(8,128)(2,1)S(1)}, bf16[3,96,512]{2,1,0:T(8,128)(2,1)S(1)}, u32[]{:S(2)}, u32[]{:S(2)}) collective-permute-start(bf16[3,96,512]{2,1,0:T(8,128)(2,1)S(1)} %pad_maximum_fusion.7), channel_id=1, source_target_pairs={{0,4},{1,3},{2,6},{3,1},{4,0},{5,7},{6,2},{7,5},{8,12},{9,11},{10,... | collective-permute-start | bytes 884744 | tf_op jit(solution)/shard_map/ppermute | solution.py:45
  57.5 23.6 %copy-start.8 = (bf16[2,304,768]{2,1,0:T(8,128)(2,1)S(1)}, bf16[2,304,768]{2,1,0:T(8,128)(2,1)}, u32[]{:S(2)}) copy-start(bf16[2,304,768]{2,1,0:T(8,128)(2,1)} %copy.43) | copy-start | bytes 2801668
  57.5 23.6 %copy-start.18 = (f32[768]{0:T(1024)S(1)}, f32[768]{0:T(1024)}, u32[]{:S(2)}) copy-start(f32[768]{0:T(1024)} %param.20) | copy-start | bytes 9220
  57.5 23.6 %copy-start.19 = (f32[768]{0:T(1024)S(1)}, f32[768]{0:T(1024)}, u32[]{:S(2)}) copy-start(f32[768]{0:T(1024)} %param.21) | copy-start | bytes 9220
  64.2 24.5 %collective-permute-start.8 = (bf16[6,96,768]{2,1,0:T(8,128)(2,1)S(1)}, bf16[6,96,768]{2,1,0:T(8,128)(2,1)S(1)}, u32[]{:S(2)}, u32[]{:S(2)}) collective-permute-start(bf16[6,96,768]{2,1,0:T(8,128)(2,1)S(1)} %pad_maximum_fusion.1.refs_11_.refs_16_), channel_id=1, source_target_pairs={{0,2},{1,5},{2,0},{3,7},{4,6},{5,1},{6,4},{7,3},{8,10},{9,13},{10,... | collective-permute-start | bytes 2654216 | tf_op jit(solution)/shard_map/ppermute | solution.py:45
  65.8 11.6 %collective-permute-start.12 = (f32[2,768]{1,0:T(2,128)S(1)}, f32[2,768]{1,0:T(2,128)}, u32[]{:S(2)}, u32[]{:S(2)}) collective-permute-start(f32[2,768]{1,0:T(2,128)S(1)} %pad_maximum_fusion.12), channel_id=1, source_target_pairs={{0,2},{1,3},{2,0},{3,1},{4,6},{5,7},{6,4},{7,5},{8,10},{9,11},{10,... | collective-permute-start | bytes 18440 | tf_op jit(solution)/shard_map/ppermute | solution.py:45
  77.4 6.7 %collective-permute-start.1 = (bf16[2,96,768]{2,1,0:T(8,128)(2,1)S(1)}, bf16[2,96,768]{2,1,0:T(8,128)(2,1)S(1)}, u32[]{:S(2)}, u32[]{:S(2)}) collective-permute-start(bf16[2,96,768]{2,1,0:T(8,128)(2,1)S(1)} %pad_maximum_fusion.6.refs_7_.refs_12_), channel_id=1, source_target_pairs={{0,2},{1,5},{2,0},{3,7},{4,6},{5,1},{6,4},{7,3},{8,10},{9,13},{10,... | collective-permute-start | bytes 884744 | tf_op jit(solution)/shard_map/ppermute | solution.py:45
  78.9 5.2 %collective-permute-start.2 = (bf16[2,96,768]{2,1,0:T(8,128)(2,1)S(1)}, bf16[2,96,768]{2,1,0:T(8,128)(2,1)S(1)}, u32[]{:S(2)}, u32[]{:S(2)}) collective-permute-start(bf16[2,96,768]{2,1,0:T(8,128)(2,1)S(1)} %pad_maximum_fusion.6.refs_7_.refs_12_), channel_id=1, source_target_pairs={{0,1},{1,0},{2,3},{3,2},{4,5},{5,4},{6,7},{7,6},{8,9},{9,8},{10,11... | collective-permute-start | bytes 884744 | tf_op jit(solution)/shard_map/ppermute | solution.py:45
  78.9 9.8 %collective-permute-start.25 = (bf16[2,96,1024]{2,1,0:T(8,128)(2,1)S(1)}, bf16[2,96,1024]{2,1,0:T(8,128)(2,1)}, u32[]{:S(2)}, u32[]{:S(2)}) collective-permute-start(bf16[2,96,1024]{2,1,0:T(8,128)(2,1)S(1)} %pad_maximum_fusion.5.refs_6_), channel_id=1, source_target_pairs={{0,2},{1,5},{2,0},{3,7},{4,6},{5,1},{6,4},{7,3},{8,10},{9,13},{10,... | collective-permute-start | bytes 1179656 | tf_op jit(solution)/shard_map/ppermute | solution.py:45
  79.5 27.9 %collective-permute-start.32 = (bf16[6,96,1024]{2,1,0:T(8,128)(2,1)}, bf16[6,96,1024]{2,1,0:T(8,128)(2,1)}, u32[]{:S(2)}, u32[]{:S(2)}) collective-permute-start(bf16[6,96,1024]{2,1,0:T(8,128)(2,1)} %pad_maximum_fusion.refs_10_), channel_id=1, source_target_pairs={{0,2},{1,5},{2,0},{3,7},{4,6},{5,1},{6,4},{7,3},{8,10},{9,13},{10,... | collective-permute-start | bytes 3538952 | tf_op jit(solution)/shard_map/ppermute | solution.py:45
  84.1 2.4 %collective-permute-start.16 = (bf16[2,96,512]{2,1,0:T(8,128)(2,1)}, bf16[2,96,512]{2,1,0:T(8,128)(2,1)S(1)}, u32[]{:S(2)}, u32[]{:S(2)}) collective-permute-start(bf16[2,96,512]{2,1,0:T(8,128)(2,1)} %collective-permute-done.14.refs_5_), channel_id=1, source_target_pairs={{0,1},{1,0},{2,3},{3,2},{4,5},{5,4},{6,7},{7,6},{8,9},{9,8},{10,11... | collective-permute-start | bytes 589832 | tf_op jit(solution)/shard_map/ppermute | solution.py:45
  84.8 6.5 %collective-permute-start.3 = (bf16[2,96,768]{2,1,0:T(8,128)(2,1)S(1)}, bf16[2,96,768]{2,1,0:T(8,128)(2,1)}, u32[]{:S(2)}, u32[]{:S(2)}) collective-permute-start(bf16[2,96,768]{2,1,0:T(8,128)(2,1)S(1)} %collective-permute-done.1.refs_8_.refs_13_), channel_id=1, source_target_pairs={{0,1},{1,0},{2,3},{3,2},{4,5},{5,4},{6,7},{7,6},{8,9},{9,8},{10,11... | collective-permute-start | bytes 884744 | tf_op jit(solution)/shard_map/ppermute | solution.py:45
  87.2 20.2 %collective-permute-start.21 = (bf16[6,96,512]{2,1,0:T(8,128)(2,1)S(1)}, bf16[6,96,512]{2,1,0:T(8,128)(2,1)}, u32[]{:S(2)}, u32[]{:S(2)}) collective-permute-start(bf16[6,96,512]{2,1,0:T(8,128)(2,1)S(1)} %pad_maximum_fusion.2.refs_8_), channel_id=1, source_target_pairs={{0,2},{1,5},{2,0},{3,7},{4,6},{5,1},{6,4},{7,3},{8,10},{9,13},{10,... | collective-permute-start | bytes 1769480 | tf_op jit(solution)/shard_map/ppermute | solution.py:45
  88.7 26.7 %collective-permute-start.9 = (bf16[6,96,768]{2,1,0:T(8,128)(2,1)S(1)}, bf16[6,96,768]{2,1,0:T(8,128)(2,1)}, u32[]{:S(2)}, u32[]{:S(2)}) collective-permute-start(bf16[6,96,768]{2,1,0:T(8,128)(2,1)S(1)} %pad_maximum_fusion.1.refs_11_.refs_16_), channel_id=1, source_target_pairs={{0,1},{1,0},{2,3},{3,2},{4,5},{5,4},{6,7},{7,6},{8,9},{9,8},{10,11... | collective-permute-start | bytes 2654216 | tf_op jit(solution)/shard_map/ppermute | solution.py:45
  88.7 27.2 %collective-permute-start.10 = (bf16[6,96,768]{2,1,0:T(8,128)(2,1)S(1)}, bf16[6,96,768]{2,1,0:T(8,128)(2,1)}, u32[]{:S(2)}, u32[]{:S(2)}) collective-permute-start(bf16[6,96,768]{2,1,0:T(8,128)(2,1)S(1)} %collective-permute-done.8.refs_12_.refs_17_), channel_id=1, source_target_pairs={{0,1},{1,0},{2,3},{3,2},{4,5},{5,4},{6,7},{7,6},{8,9},{9,8},{10,11... | collective-permute-start | bytes 2654216 | tf_op jit(solution)/shard_map/ppermute | solution.py:45
  91.3 23.2 %collective-permute-start.22 = (bf16[6,96,512]{2,1,0:T(8,128)(2,1)S(1)}, bf16[6,96,512]{2,1,0:T(8,128)(2,1)}, u32[]{:S(2)}, u32[]{:S(2)}) collective-permute-start(bf16[6,96,512]{2,1,0:T(8,128)(2,1)S(1)} %pad_maximum_fusion.2.refs_8_), channel_id=1, source_target_pairs={{0,1},{1,0},{2,3},{3,2},{4,5},{5,4},{6,7},{7,6},{8,9},{9,8},{10,11... | collective-permute-start | bytes 1769480 | tf_op jit(solution)/shard_map/ppermute | solution.py:45
  107.4 44.9 %collective-permute-start.33 = (bf16[6,96,1024]{2,1,0:T(8,128)(2,1)}, bf16[6,96,1024]{2,1,0:T(8,128)(2,1)}, u32[]{:S(2)}, u32[]{:S(2)}) collective-permute-start(bf16[6,96,1024]{2,1,0:T(8,128)(2,1)} %pad_maximum_fusion.refs_10_), channel_id=1, source_target_pairs={{0,1},{1,0},{2,3},{3,2},{4,5},{5,4},{6,7},{7,6},{8,9},{9,8},{10,11... | collective-permute-start | bytes 3538952 | tf_op jit(solution)/shard_map/ppermute | solution.py:45
  107.4 44.9 %collective-permute-start.34 = (bf16[6,96,1024]{2,1,0:T(8,128)(2,1)}, bf16[6,96,1024]{2,1,0:T(8,128)(2,1)}, u32[]{:S(2)}, u32[]{:S(2)}) collective-permute-start(bf16[6,96,1024]{2,1,0:T(8,128)(2,1)} %collective-permute-done.32.refs_11_), channel_id=1, source_target_pairs={{0,1},{1,0},{2,3},{3,2},{4,5},{5,4},{6,7},{7,6},{8,9},{9,8},{10,11... | collective-permute-start | bytes 3538952 | tf_op jit(solution)/shard_map/ppermute | solution.py:45
  114.6 24.5 %collective-permute-start.23 = (bf16[6,96,512]{2,1,0:T(8,128)(2,1)}, bf16[6,96,512]{2,1,0:T(8,128)(2,1)S(1)}, u32[]{:S(2)}, u32[]{:S(2)}) collective-permute-start(bf16[6,96,512]{2,1,0:T(8,128)(2,1)} %collective-permute-done.21.refs_9_), channel_id=1, source_target_pairs={{0,1},{1,0},{2,3},{3,2},{4,5},{5,4},{6,7},{7,6},{8,9},{9,8},{10,11... | collective-permute-start | bytes 1769480 | tf_op jit(solution)/shard_map/ppermute | solution.py:45
  115.4 36.9 %collective-permute-start.26 = (bf16[2,96,1024]{2,1,0:T(8,128)(2,1)S(1)}, bf16[2,96,1024]{2,1,0:T(8,128)(2,1)S(1)}, u32[]{:S(2)}, u32[]{:S(2)}) collective-permute-start(bf16[2,96,1024]{2,1,0:T(8,128)(2,1)S(1)} %pad_maximum_fusion.5.refs_6_), channel_id=1, source_target_pairs={{0,1},{1,0},{2,3},{3,2},{4,5},{5,4},{6,7},{7,6},{8,9},{9,8},{10,11... | collective-permute-start | bytes 1179656 | tf_op jit(solution)/shard_map/ppermute | solution.py:45
  115.9 36.3 %collective-permute-start.27 = (bf16[2,96,1024]{2,1,0:T(8,128)(2,1)}, bf16[2,96,1024]{2,1,0:T(8,128)(2,1)S(1)}, u32[]{:S(2)}, u32[]{:S(2)}) collective-permute-start(bf16[2,96,1024]{2,1,0:T(8,128)(2,1)} %collective-permute-done.25.refs_7_), channel_id=1, source_target_pairs={{0,1},{1,0},{2,3},{3,2},{4,5},{5,4},{6,7},{7,6},{8,9},{9,8},{10,11... | collective-permute-start | bytes 1179656 | tf_op jit(solution)/shard_map/ppermute | solution.py:45
  116.0 23.0 %copy-start.4 = (bf16[2,96,512]{2,1,0:T(8,128)(2,1)S(1)}, bf16[2,96,512]{2,1,0:T(8,128)(2,1)}, u32[]{:S(2)}) copy-start(bf16[2,96,512]{2,1,0:T(8,128)(2,1)} %copy-done.3) | copy-start | bytes 589828
  116.0 23.0 %copy-start.6 = (bf16[2,96,512]{2,1,0:T(8,128)(2,1)S(1)}, bf16[2,96,512]{2,1,0:T(8,128)(2,1)}, u32[]{:S(2)}) copy-start(bf16[2,96,512]{2,1,0:T(8,128)(2,1)} %copy-done.5) | copy-start | bytes 589828
  199.8 21.3 %copy-start.9 = (bf16[2,297,768]{2,1,0:T(8,128)(2,1)S(1)}, bf16[2,297,768]{2,1,0:T(8,128)(2,1)}, u32[]{:S(2)}) copy-start(bf16[2,297,768]{2,1,0:T(8,128)(2,1)} %get-tuple-element.34) | copy-start | bytes 2737156
  199.8 1.6 collective-permute-start.35
  201.4 4.7 %collective-permute-start.36 = (bf16[100,384]{1,0:T(8,128)(2,1)S(1)}, bf16[100,384]{1,0:T(8,128)(2,1)S(1)}, u32[]{:S(2)}, u32[]{:S(2)}) collective-permute-start(bf16[100,384]{1,0:T(8,128)(2,1)S(1)} %get-tuple-element.39), channel_id=1, source_target_pairs={{0,4},{1,5},{2,6},{3,7},{4,0},{5,1},{6,2},{7,3},{8,12},{9,13},{10,... | collective-permute-start | bytes 230408 | tf_op jit(solution)/shard_map/ppermute | solution.py:45
  206.2 4.5 %collective-permute-start.37 = (bf16[100,384]{1,0:T(8,128)(2,1)S(1)}, bf16[100,384]{1,0:T(8,128)(2,1)S(1)}, u32[]{:S(2)}, u32[]{:S(2)}) collective-permute-start(bf16[100,384]{1,0:T(8,128)(2,1)S(1)} %fusion.2), channel_id=1, source_target_pairs={{0,2},{1,3},{2,0},{3,1},{4,6},{5,7},{6,4},{7,5},{8,10},{9,11},{10,... | collective-permute-start | bytes 230408 | tf_op jit(solution)/shard_map/ppermute | solution.py:45
  210.7 4.5 %collective-permute-start.38 = (bf16[100,384]{1,0:T(8,128)(2,1)S(1)}, bf16[100,384]{1,0:T(8,128)(2,1)S(1)}, u32[]{:S(2)}, u32[]{:S(2)}) collective-permute-start(bf16[100,384]{1,0:T(8,128)(2,1)S(1)} %fusion.6), channel_id=1, source_target_pairs={{0,8},{1,9},{2,10},{3,11},{4,12},{5,13},{6,14},{7,15},{8,0},{9,1},... | collective-permute-start | bytes 230408 | tf_op jit(solution)/shard_map/ppermute | solution.py:45
  215.3 5.7 %collective-permute-start.39 = (bf16[100,384]{1,0:T(8,128)(2,1)S(1)}, bf16[100,384]{1,0:T(8,128)(2,1)S(1)}, u32[]{:S(2)}, u32[]{:S(2)}) collective-permute-start(bf16[100,384]{1,0:T(8,128)(2,1)S(1)} %fusion.3), channel_id=1, source_target_pairs={{0,16},{1,17},{2,18},{3,19},{4,20},{5,21},{6,22},{7,23},{8,24},{9,... | collective-permute-start | bytes 230408 | tf_op jit(solution)/shard_map/ppermute | solution.py:45
  221.0 3.0 %collective-permute-start.40 = (bf16[100,384]{1,0:T(8,128)(2,1)S(1)}, bf16[100,384]{1,0:T(8,128)(2,1)S(1)}, u32[]{:S(2)}, u32[]{:S(2)}) collective-permute-start(bf16[100,384]{1,0:T(8,128)(2,1)S(1)} %get-tuple-element.37), channel_id=1, source_target_pairs={{0,1},{1,0},{2,3},{3,2},{4,5},{5,4},{6,7},{7,6},{8,9},{9,8},{10,11... | collective-permute-start | bytes 230408 | tf_op jit(solution)/shard_map/ppermute | solution.py:45
  (17 other events, 97.3 us)
